TPU v7x, 32 devices: a whole 2x2x4 slice. The times are simulated.
32 devices in a mesh: frame: 4 (over x, core), within: 8 (over z, y).
Axes of the slice: x: 2, y: 2, z: 4, core: 2. Of those that a mesh axis runs over, the one named last changes fastest.
Arguments:
- queries: bfloat16 [4, 576, 1024], P('frame', 'within'), may hold values from -6 to 6
- keys_in: bfloat16 [4, 576, 1024], P('frame', 'within'), may hold values from -6 to 6
- values_in: bfloat16 [4, 576, 1024], P('frame', 'within'), may hold values from -6 to 6
- grad_out: bfloat16 [4, 576, 1024], P('frame', 'within'), may hold values from -6 to 6
- partners: int32 [4, 2], replicated, may hold values from 0 to 3
- registers: int32 [4], replicated, may hold values from 1 to 144
Outputs:
- grad_queries: bfloat16 [4, 576, 1024], P('frame', 'within')
- grad_keys: bfloat16 [4, 576, 1024], P('frame', 'within')
- grad_values: bfloat16 [4, 576, 1024], P('frame', 'within')
Inputs may be any that keep to these rules, and one draw needn't show every extreme that they name: `partners`: A row may list a group more than once, and may list its own group.
All inputs are finite; a program needn't handle non-finite values.
Results may differ from a plain program's by a relative error of at most 0.012.
Values may be sent and summed in bfloat16 or wider, within the bound.
A program may use at most 128 MiB of HBM per device.

v0:
```python
import functools
import math

import jax
import jax.numpy as jnp
import numpy as np
from jax import lax
from jax.experimental import pallas as pl
from jax.experimental.pallas import tpu as pltpu
from jax.sharding import PartitionSpec as P

DH = 64
PAIR = 2 * DH
SPLITS = 3
UNIT = 640
HIDDEN = -1e30
BF = jnp.bfloat16
F32 = jnp.float32
MESH = pl.DeviceIdType.MESH


def pieces_of(value):
    left, out = float(value), []
    for _ in range(SPLITS):
        part = float(np.asarray(left, dtype=jnp.bfloat16))
        out.append(part)
        left = left - part if abs(value) < 1e20 else 0.0
    return out


def rdot(a, b):
    return lax.dot_general(a, b, (((1,), (1,)), ((), ())), preferred_element_type=F32)


def dot(a, b):
    return jnp.dot(a, b, preferred_element_type=F32)


def each(lo, hi, do):
    def step(t, carry):
        do(t)
        return carry
    lax.fori_loop(lo, hi, step, 0)


def kernel(F, W, R, QC, inline, part_ref, reg_ref, q_ref, k_ref, v_ref, d_ref, dq_in, fin_in,
           kv_send, qd_send, kv_in, qd_in, kaug, vz, kt, qaug, xraw, qdz, sbuf, dpbuf, acc, dqacc, dqs,
           tops, top_ref, total_ref, dsum_ref,
           red_send, red_in, fin_send, dq_send, own_sem,
           kv_ss, fw_ss, kv_rs, qd_ss, qd_rs, red_ss, red_rs, fin_ss, fin_rs, dq_ss, dq_rs):
    fs = F // R
    hf = F // 2
    rows = q_ref.shape[1]
    width = q_ref.shape[2]
    seq = rows * W
    n_slots = part_ref.shape[0]
    scale = DH ** -0.5
    half = dq_send.shape[2]
    nq = R * seq
    n_chunks = nq // QC
    n_units, per = acc.shape[0], acc.shape[1]
    unit = per * F * rows
    f = lax.axis_index("frame")
    w = lax.axis_index("within")
    c = lax.rem(f, fs)
    a0 = lax.div(f, fs)
    sib = f + 1 - 2 * lax.rem(f, 2)
    head = w * R + a0

    barrier = pltpu.get_barrier_semaphore()

    def ahead(dw):
        return lax.rem(w + W - dw, W)

    def behind(dw):
        return lax.rem(w + dw, W)

    def greet(t):
        pl.semaphore_signal(barrier, inc=1, device_id=(lax.rem(f + 2 * lax.rem(t, hf), F), ahead(lax.div(t, hf))),
                            device_id_type=MESH)

    each(1, hf * W, greet)
    for dc in range(1, fs, 2):
        pl.semaphore_signal(barrier, inc=1, device_id=(a0 * fs + lax.rem(c + dc, fs), w), device_id_type=MESH)

    for first, second, out in ((q_ref, d_ref, qd_send), (k_ref, v_ref, kv_send)):
        for j in range(width // PAIR):
            cols = slice(j * PAIR, (j + 1) * PAIR)
            one = first[0, :, cols]
            two = second[0, :, cols]
            out[2 * j] = jnp.concatenate([one[:, :DH], two[:, :DH]], axis=1)
            out[2 * j + 1] = jnp.concatenate([one[:, DH:], two[:, DH:]], axis=1)
    kv_in[f, w] = kv_send[head]
    qd_in[a0, w] = qd_send[head]

    pl.semaphore_wait(barrier, hf * W - 1 + fs // 2)

    def kv_copy(t):
        ff = lax.rem(f + 2 * lax.rem(t, hf), F)
        ww = ahead(lax.div(t, hf))
        return pltpu.make_async_remote_copy(
            src_ref=kv_send.at[ww * R + lax.div(ff, fs)], dst_ref=kv_in.at[f, w],
            send_sem=kv_ss.at[t], recv_sem=kv_rs.at[f * W + w],
            device_id=(ff, ww), device_id_type=MESH)

    def pass_on(origin, t):
        ff = lax.rem(origin + F - 2 * lax.rem(t, hf), F)
        ww = behind(lax.div(t, hf))
        return pltpu.make_async_remote_copy(
            src_ref=kv_in.at[ff, ww], dst_ref=kv_in.at[ff, ww],
            send_sem=fw_ss.at[t], recv_sem=kv_rs.at[ff * W + ww],
            device_id=(sib, w), device_id_type=MESH)

    def qd_copy(t):
        aa, ww = lax.rem(a0 + lax.rem(t, R), R), ahead(lax.div(t, R))
        return pltpu.make_async_remote_copy(
            src_ref=qd_send.at[ww * R + aa], dst_ref=qd_in.at[a0, w],
            send_sem=qd_ss.at[t], recv_sem=qd_rs.at[a0 * W + w],
            device_id=(aa * fs + c, ww), device_id_type=MESH)

    def arrival(t, buffer, send, recv, index, source):
        return pltpu.make_async_remote_copy(
            src_ref=buffer.at[index], dst_ref=buffer.at[index], send_sem=send.at[t], recv_sem=recv,
            device_id=source, device_id_type=MESH)

    def qd_arrival(t):
        aa, ww = lax.rem(a0 + R - lax.rem(t, R), R), behind(lax.div(t, R))
        return arrival(t, qd_in, qd_ss, qd_rs.at[aa * W + ww], (aa, ww), (aa * fs + c, ww))

    def head_arrival(t, buffer, send, recv):
        aa, ww = lax.rem(a0 + R - lax.rem(t, R), R), ahead(lax.div(t, R))
        return arrival(t, buffer, send, recv.at[ww * R + aa], (ww * R + aa,), (aa * fs + c, ww))

    each(1, R * W, lambda t: qd_copy(t).start())
    pass_on(f, 0).start()
    each(1, hf * W, lambda t: kv_copy(t).start())

    acc[...] = jnp.zeros_like(acc)
    dqacc[...] = jnp.zeros_like(dqacc)

    def relay(t):
        move = pass_on(f, t)
        move.wait_recv()
        move.start()

    lane1 = lax.broadcasted_iota(jnp.int32, (1, PAIR), 1)
    table = [pieces_of(HIDDEN)] + [pieces_of(math.log(n)) for n in range(1, n_slots + 2)]
    marks = []
    for p in range(F):
        seen = jnp.zeros((1, PAIR), F32)
        unseen = jnp.zeros((1, PAIR), F32)
        for gi in range(R):
            g = c + fs * gi
            own = jnp.where(p == g, 1, 0)
            count = own
            for slot in range(n_slots):
                count = count + jnp.where(part_ref[slot, g] == p, 1, 0)
            for e in range(SPLITS):
                here = lane1 == DH + SPLITS * gi + e
                for n in range(n_slots + 2):
                    if n < 2:
                        unseen = jnp.where(here & (own == n), table[n][e], unseen)
                    seen = jnp.where(here & (count == n), table[n][e], seen)
        marks.append((seen, unseen))

    lane = lax.broadcasted_iota(jnp.int32, (rows, PAIR), 1)
    row = lax.broadcasted_iota(jnp.int32, (rows, PAIR), 0)

    def prepare(u):
        aug, raw = [], []
        for d in range(per):
            ww = behind(u * per + d)
            for p in range(F):
                both = kv_in[p, ww].astype(F32)
                extra = jnp.where(row + ww * rows >= reg_ref[p], marks[p][0], marks[p][1])
                raw.append(both)
                aug.append(jnp.where(lane < DH, both, extra))
        raw = jnp.concatenate(raw, axis=0)
        keep = lax.broadcasted_iota(jnp.int32, (unit, PAIR), 1) >= DH
        kaug[u] = jnp.concatenate(aug, axis=0).astype(BF)
        vz[u] = jnp.where(keep, raw, 0.0).astype(BF)
        kt[u] = (raw * scale).T[:DH].astype(BF)

    def direct(u):
        each(max(u * per * hf, 1), (u + 1) * per * hf, relay)

    def settle(u):
        each(u * per * hf, (u + 1) * per * hf, lambda t: pass_on(sib, t).wait_recv())
        prepare(u)

    def rows_of(i):
        return pl.ds(pl.multiple_of(i * QC, QC), QC)

    def begin(b):
        top_ref[b] = jnp.full_like(top_ref[b], -3e38)
        total_ref[b] = jnp.zeros_like(total_ref[b])
        dsum_ref[b] = jnp.zeros_like(dsum_ref[b])

    def forth(u, i, b):
        at = rows_of(i)
        raw = rdot(kaug[u], qaug[at])
        old = top_ref[b]
        top = jnp.maximum(old, jnp.max(raw, axis=0, keepdims=True))
        keep = jnp.exp(old - top)
        expo = jnp.exp(raw - top)
        dprod = rdot(vz[u], xraw[at])
        sbuf[u, b] = expo
        dpbuf[u, b] = dprod
        tops[u, b] = top
        top_ref[b] = top
        total_ref[b] = total_ref[b] * keep + jnp.sum(expo, axis=0, keepdims=True)
        dsum_ref[b] = dsum_ref[b] * keep + jnp.sum(expo * dprod, axis=0, keepdims=True)

    def back(u, i, b):
        inv = 1.0 / total_ref[b]
        factor = jnp.exp(tops[u, b] - top_ref[b]) * inv
        prob = sbuf[u, b] * factor
        dscore = (prob * (dpbuf[u, b] - dsum_ref[b] * inv)).astype(BF)
        added = dot(jnp.concatenate([dscore, prob.astype(BF)], axis=1), qdz[i])
        acc[u] += added.reshape(per, F, rows, PAIR)
        dqacc[i] += dot(kt[u], dscore)

    def own_copy(block, buffer, n):
        return pltpu.make_async_copy(block, buffer.at[head], own_sem.at[n])

    def red_copy(u, dc):
        return pltpu.make_async_remote_copy(
            src_ref=red_send.at[u, dc - 1], dst_ref=red_in.at[u, dc - 1],
            send_sem=red_ss.at[u * (fs - 1) + dc - 1], recv_sem=red_rs.at[u * (fs - 1) + dc - 1],
            device_id=(a0 * fs + lax.rem(c + dc, fs), w), device_id_type=MESH)

    def ship_part(u):
        for dc in range(1, fs):
            for gi in range(R):
                red_send[u, dc - 1, gi] = acc[u, :, lax.rem(c + dc, fs) + fs * gi].astype(BF)
            red_copy(u, dc).start()

    def fin_copy(t):
        dw = lax.div(t, R)
        aa, ww = lax.rem(a0 + lax.rem(t, R), R), behind(dw)
        return pltpu.make_async_remote_copy(
            src_ref=fin_send.at[lax.div(dw, per), aa, lax.rem(dw, per)], dst_ref=fin_in.at[head],
            send_sem=fin_ss.at[t], recv_sem=fin_rs.at[head],
            device_id=(aa * fs + c, ww), device_id_type=MESH)

    def ship_home(u):
        for dc in range(1, fs):
            red_copy(u, dc).wait_recv()
        for gi in range(R):
            whole = acc[u, :, c + fs * gi]
            for dc in range(1, fs):
                whole = whole + red_in[u, dc - 1, gi].astype(F32)
            fin_send[u, gi] = whole.astype(BF)
        if u == 0:
            own_copy(fin_send.at[0, a0, 0], fin_in, 0).start()
        each(max(u * per * R, 1), (u + 1) * per * R, lambda t: fin_copy(t).start())

    def take_queries():
        each(1, R * W, lambda t: qd_arrival(t).wait_recv())
        wide = lax.broadcasted_iota(jnp.int32, (nq, PAIR), 1)
        tall = lax.broadcasted_iota(jnp.int32, (nq, PAIR), 0)
        both = qd_in[...].astype(F32).reshape(nq, PAIR)
        mark = jnp.zeros((nq, PAIR), F32)
        for gi in range(R):
            mine = (tall >= gi * seq) & (tall < (gi + 1) * seq)
            mark = jnp.where(mine & (wide >= DH + SPLITS * gi) & (wide < DH + SPLITS * (gi + 1)), 1.0, mark)
        scaled = both * scale
        qaug[...] = jnp.where(wide < DH, scaled, mark).astype(BF)
        xraw[...] = both.astype(BF)
        qdz[:, :QC] = jnp.where(wide < DH, scaled, 0.0).astype(BF).reshape(n_chunks, QC, PAIR)
        qdz[:, QC:] = jnp.where(wide >= DH, both, 0.0).astype(BF).reshape(n_chunks, QC, PAIR)

    take_queries()
    if inline:
        each(0, n_chunks, begin)
        direct(0)
        for u in range(n_units):
            settle(u)
            forth(u, 0, 0)
            if u + 1 < n_units:
                direct(u + 1)
            each(1, n_chunks, lambda i: forth(u, i, i))
        for u in range(n_units):
            back(u, 0, 0)
            if u:
                ship_home(u - 1)
            each(1, n_chunks, lambda i: back(u, i, i))
            ship_part(u)
    else:
        for u in range(n_units):
            direct(u)
        for u in range(n_units):
            settle(u)

        def block(i):
            begin(0)
            each(0, n_units, lambda u: forth(u, i, 0))
            each(0, n_units, lambda u: back(u, i, 0))

        each(0, n_chunks, block)
        for u in range(n_units):
            ship_part(u)
        for u in range(n_units - 1):
            ship_home(u)

    def dq_copy(t):
        aa, ww = lax.rem(a0 + lax.rem(t, R), R), behind(lax.div(t, R))
        return pltpu.make_async_remote_copy(
            src_ref=dq_send.at[aa, ww], dst_ref=dq_in.at[head],
            send_sem=dq_ss.at[t], recv_sem=dq_rs.at[head],
            device_id=(aa * fs + c, ww), device_id_type=MESH)

    for i in range(n_chunks):
        dqs[i * QC:(i + 1) * QC] = jnp.concatenate([dqacc[i], jnp.zeros((DH, QC), F32)], axis=0).T
    for gi in range(R):
        for ww in range(W):
            base = gi * seq + ww * rows
            dq_send[gi, ww] = jnp.concatenate(
                [dqs[base:base + half, :DH], dqs[base + rows - half:base + rows, :DH]], axis=1).astype(BF)
    own_copy(dq_send.at[a0, w], dq_in, 1).start()
    each(1, R * W, lambda t: dq_copy(t).start())
    ship_home(n_units - 1)

    each(1, R * W, lambda t: head_arrival(t, dq_in, dq_ss, dq_rs).wait_recv())
    each(1, R * W, lambda t: head_arrival(t, fin_in, fin_ss, fin_rs).wait_recv())
    each(1, hf * W, lambda t: kv_copy(t).wait_send())
    each(0, hf * W, lambda t: pass_on(f, t).wait_send())
    each(1, R * W, lambda t: qd_copy(t).wait_send())
    own_copy(fin_send.at[0, a0, 0], fin_in, 0).wait()
    own_copy(dq_send.at[a0, w], dq_in, 1).wait()
    each(1, R * W, lambda t: dq_copy(t).wait_send())
    each(1, R * W, lambda t: fin_copy(t).wait_send())
    for u in range(n_units):
        for dc in range(1, fs):
            red_copy(u, dc).wait_send()


def tokens_again(dq_in, fin_in, dq_out, dk_out, dv_out):
    half, rows, width = dq_in.shape[1], dq_out.shape[1], dq_out.shape[2]
    for j in range(width // PAIR):
        cols = slice(j * PAIR, (j + 1) * PAIR)
        sides = []
        for h in (2 * j, 2 * j + 1):
            got = dq_in[h].astype(F32)
            sides.append(jnp.concatenate([got[:, :DH], got[2 * half - rows:, DH:]], axis=0))
        dq_out[0, :, cols] = jnp.concatenate(sides, axis=1).astype(BF)

    for j in range(width // PAIR):
        cols = slice(j * PAIR, (j + 1) * PAIR)
        one, two = fin_in[2 * j], fin_in[2 * j + 1]
        dk_out[0, :, cols] = jnp.concatenate([one[:, :DH], two[:, :DH]], axis=1)
        dv_out[0, :, cols] = jnp.concatenate([one[:, DH:], two[:, DH:]], axis=1)


def local(F, W, queries, keys_in, values_in, grad_out, partners, registers):
    _, rows, width = queries.shape
    heads = width // DH
    R = heads // W
    fs = F // R
    seq = rows * W
    nq = R * seq
    half = ((rows + 1) // 2 + 7) // 8 * 8
    inline = F * seq * nq * 8 <= 24 * 2 ** 20
    QC = next(b for b in ((576, 384, 128) if inline else (128,)) if nq % b == 0)
    held = nq // QC if inline else 1
    per = next(n for n in range(W, 0, -1) if W % n == 0 and (n == 1 or n * F * rows <= UNIT))
    units = W // per
    unit = per * F * rows
    vm = lambda *shape: pltpu.VMEM(shape, BF)
    vf = lambda *shape: pltpu.VMEM(shape, F32)
    dma = lambda n: pltpu.SemaphoreType.DMA((n,))
    out = jax.ShapeDtypeStruct((1, rows, width), BF)
    dq_heads, kv_heads = pl.pallas_call(
        functools.partial(kernel, F, W, R, QC, inline),
        out_shape=(jax.ShapeDtypeStruct((heads, half, PAIR), BF), jax.ShapeDtypeStruct((heads, rows, PAIR), BF)),
        in_specs=[pl.BlockSpec(memory_space=pltpu.SMEM)] * 2 + [pl.BlockSpec(memory_space=pltpu.VMEM)] * 4,
        out_specs=(pl.BlockSpec(memory_space=pl.ANY),) * 2,
        scratch_shapes=[
            vm(heads, rows, PAIR), vm(heads, rows, PAIR),
            vm(F, W, rows, PAIR), vm(R, W, rows, PAIR),
            vm(units, unit, PAIR), vm(units, unit, PAIR), vm(units, DH, unit),
            vm(nq, PAIR), vm(nq, PAIR), vm(nq // QC, 2 * QC, PAIR),
            vf(units, held, unit, QC), vf(units, held, unit, QC), vf(units, per, F, rows, PAIR),
            vf(nq // QC, DH, QC), vf(nq, PAIR),
            vf(units, held, 1, QC), vf(held, 1, QC), vf(held, 1, QC), vf(held, 1, QC),
            vm(units, fs - 1, R, per, rows, PAIR), vm(units, fs - 1, R, per, rows, PAIR),
            vm(units, R, per, rows, PAIR), vm(R, W, half, PAIR), dma(2),
            dma(F // 2 * W), dma(F // 2 * W), dma(F * W), dma(R * W), dma(R * W),
            dma(units * (fs - 1)), dma(units * (fs - 1)), dma(R * W), dma(heads), dma(R * W), dma(heads),
        ],
        compiler_params=pltpu.CompilerParams(
            collective_id=0, has_side_effects=True, vmem_limit_bytes=60 * 2 ** 20),
    )(partners.T, registers, queries, keys_in, values_in, grad_out)
    return pl.pallas_call(
        tokens_again,
        out_shape=(out, out, out),
        in_specs=[pl.BlockSpec(memory_space=pltpu.VMEM)] * 2,
        out_specs=(pl.BlockSpec(memory_space=pltpu.VMEM),) * 3,
    )(dq_heads, kv_heads)


def solution(mesh):
    spec = P("frame", "within", None)
    return jax.shard_map(
        functools.partial(local, mesh.shape["frame"], mesh.shape["within"]),
        mesh=mesh,
        in_specs=(spec, spec, spec, spec, P(), P()),
        out_specs=(spec, spec, spec),
        check_vma=False,
    )
```

profile of v0, /device:TPU:0, one launch (start us, length us, event | category | flops | bytes accessed | tf_op | source)
XLA Modules:
  0.0 47.9 jit_solution(14455702739967276086)
XLA Ops:
  0.6 45.3 %shard_map.85 = (bf16[16,40,128]{2,1,0:T(8,128)(2,1)}, bf16[16,72,128]{2,1,0:T(8,128)(2,1)}) custom-call(s32[2,4]{1,0:T(2,128)} %bitcast.1, s32[4]{0:T(128)} %reg_ref.1, bf16[1,72,1024]{2,1,0:T(8,128)(2,1)} %q_ref.1, bf16[1,72,1024]{2,1,0:T(8,128)(2,1)} %k_ref.1, bf16[1,72,1024]{2,1,0:T(8,128)(2,1)} %v_ref.1, bf16[1,72,1024]{2,1,0:T(8,128)(2,1)} %d_ref.1), custom_call_target="tpu_custom_call" | custom-call | tf_op jit(solution)/shard_map/pallas_call | solution.py:373
  45.9 2.0 %shard_map.86 = (bf16[1,72,1024]{2,1,0:T(8,128)(2,1)}, bf16[1,72,1024]{2,1,0:T(8,128)(2,1)}, bf16[1,72,1024]{2,1,0:T(8,128)(2,1)}) custom-call(bf16[16,40,128]{2,1,0:T(8,128)(2,1)} %get-tuple-element.5.dq_in, bf16[16,72,128]{2,1,0:T(8,128)(2,1)} %get-tuple-element.6.fin_in), custom_call_target="tpu_custom_call" | custom-call | tf_op jit(solution)/shard_map/pallas_call | solution.py:394
where the time goes:
time: 48.1 us; the launch traced here: 47.9 us
  Pallas kernels  47.3 us (98%)
  between operations  0.64 us (1%)
    pallas_call x1, Pallas kernels, local(): pl.pallas_call(functools.partial(kernel, F, W, R, QC, inline), out_shape=...  45.3 us
    pallas_call x1, Pallas kernels, local(): pl.pallas_call(tokens_again, out_shape=(out, out, out), in_specs=[pl.Bloc...  1.99 us

commit v1 on v0

--- a/solution.py
+++ b/solution.py
@@ -399,10 +399,390 @@
     )(dq_heads, kv_heads)
 
 
+def halves(F, W, part_ref, reg_ref, q_ref, k_ref, v_ref, d_ref, dq_in, fin_in,
+           kv_send, qd_send, kv_in, qd_in, kaug, vz, kt, qaug, xraw, qdz, sbuf, dpbuf, acc, dqacc, dqs,
+           tops, top_ref, total_ref, dsum_ref, st_send, st_in, fin_send, dq_send, own_sem,
+           kv_ss, kv_rs, qd_ss, qd_rs, st_ss, st_rs, dq_ss, dq_rs, fin_ss, fin_rs):
+    rows, width = q_ref.shape[1], q_ref.shape[2]
+    n_slots = part_ref.shape[0]
+    U, per = acc.shape[0], acc.shape[1]
+    L = U * per
+    heads = F * L
+    group = per * F
+    unit = group * rows
+    QC = unit
+    scale = DH ** -0.5
+    half = dq_send.shape[3]
+    f = lax.axis_index("frame")
+    w = lax.axis_index("within")
+    part = lax.div(w, L)
+    other = 1 - part
+    l = lax.rem(w, L)
+    u0 = lax.div(l, per)
+    d0 = lax.rem(l, per)
+    head = f * L + l
+
+    barrier = pltpu.get_barrier_semaphore()
+
+    def greet(t):
+        pl.semaphore_signal(barrier, inc=1, device_id=(lax.rem(f + lax.rem(t, F), F), lax.rem(w + lax.div(t, F), W)),
+                            device_id_type=MESH)
+
+    each(1, F * W, greet)
+
+    for first, second, out in ((k_ref, v_ref, kv_send), (q_ref, d_ref, qd_send)):
+        for j in range(width // PAIR):
+            cols = slice(j * PAIR, (j + 1) * PAIR)
+            one = first[0, :, cols]
+            two = second[0, :, cols]
+            out[2 * j] = jnp.concatenate([one[:, :DH], two[:, :DH]], axis=1)
+            out[2 * j + 1] = jnp.concatenate([one[:, DH:], two[:, DH:]], axis=1)
+    kv_in[l, f] = kv_send[head]
+    qd_in[w, f] = qd_send[head]
+
+    pl.semaphore_wait(barrier, F * W - 1)
+
+    def around(t):
+        return lax.rem(d0 + lax.div(lax.rem(t, group), F), per), lax.rem(f + lax.rem(t, F), F)
+
+    def near(t):
+        d, ff = around(t)
+        return ff, lax.rem(u0 + lax.div(t, group), U) * per + d
+
+    def far(t):
+        d, ff = around(lax.div(t, U))
+        return ff, lax.rem(u0 + lax.rem(t, U), U) * per + d
+
+    def remote(src, dst, ss, rs, device):
+        return pltpu.make_async_remote_copy(src_ref=src, dst_ref=dst, send_sem=ss, recv_sem=rs,
+                                            device_id=device, device_id_type=MESH)
+
+    def kv_copy(t):
+        ff, ll = near(t)
+        return remote(kv_send.at[ff * L + ll], kv_in.at[l, f], kv_ss.at[t], kv_rs.at[l * F + f], (ff, part * L + ll))
+
+    def kv_arrival(t):
+        ff, ll = near(t)
+        here = kv_in.at[ll, ff]
+        return remote(here, here, kv_ss.at[t], kv_rs.at[ll * F + ff], (ff, part * L + ll))
+
+    def qd_copy(t):
+        ff, ll = near(t)
+        return remote(qd_send.at[ff * L + ll], qd_in.at[w, f], qd_ss.at[t], qd_rs.at[w * F + f], (ff, part * L + ll))
+
+    def qd_cross(t):
+        ff, ll = far(t)
+        return remote(qd_send.at[ff * L + ll], qd_in.at[w, f], qd_ss.at[heads + t], qd_rs.at[w * F + f],
+                      (ff, other * L + ll))
+
+    def block_of(slot):
+        if slot < U:
+            return part * U + lax.rem(u0 + slot, U)
+        return other * U + (slot - U) + part * (U - 1 - 2 * (slot - U))
+
+    def qd_arrival(block, t):
+        d, ff = around(t)
+        ww = block * per + d
+        here = qd_in.at[ww, ff]
+        return remote(here, here, qd_ss.at[t], qd_rs.at[ww * F + ff], (ff, ww))
+
+    def send_near(t):
+        kv_copy(t).start()
+        qd_copy(t).start()
+
+    each(1, heads, send_near)
+    each(0, heads, lambda t: qd_cross(t).start())
+
+    acc[...] = jnp.zeros_like(acc)
+    st_send[...] = jnp.zeros_like(st_send)
+
+    lane1 = lax.broadcasted_iota(jnp.int32, (1, PAIR), 1)
+    table = [pieces_of(HIDDEN)] + [pieces_of(math.log(n)) for n in range(1, n_slots + 2)]
+    marks = []
+    for p in range(F):
+        seen = jnp.zeros((1, PAIR), F32)
+        unseen = jnp.zeros((1, PAIR), F32)
+        for g in range(F):
+            own = 1 if p == g else 0
+            count = own
+            for slot in range(n_slots):
+                count = count + jnp.where(part_ref[slot, g] == p, 1, 0)
+            for e in range(SPLITS):
+                here = lane1 == DH + SPLITS * g + e
+                unseen = jnp.where(here, table[own][e], unseen)
+                for n in range(own, n_slots + 2):
+                    seen = jnp.where(here & (count == n), table[n][e], seen)
+        marks.append((seen, unseen))
+
+    lane = lax.broadcasted_iota(jnp.int32, (rows, PAIR), 1)
+    row = lax.broadcasted_iota(jnp.int32, (rows, PAIR), 0)
+    tall = lax.broadcasted_iota(jnp.int32, (unit, PAIR), 1)
+
+    def prepare(j):
+        u = lax.rem(u0 + j, U)
+        aug, raw = [], []
+        for d in range(per):
+            ll = u * per + d
+            for p in range(F):
+                both = kv_in[ll, p].astype(F32)
+                extra = jnp.where(row + (part * L + ll) * rows >= reg_ref[p], marks[p][0], marks[p][1])
+                raw.append(both)
+                aug.append(jnp.where(lane < DH, both, extra))
+        raw = jnp.concatenate(raw, axis=0)
+        kaug[j] = jnp.concatenate(aug, axis=0).astype(BF)
+        vz[j] = jnp.where(tall >= DH, raw, 0.0).astype(BF)
+        kt[j] = (raw * scale).T[:DH].astype(BF)
+
+    def take_keys(j):
+        each(max(j * group, 1), (j + 1) * group, lambda t: kv_arrival(t).wait_recv())
+        prepare(j)
+
+    hot = [jnp.where((lane >= DH + SPLITS * g) & (lane < DH + SPLITS * (g + 1)), 1.0, 0.0) for g in range(F)]
+
+    def take_queries(i):
+        block = block_of(i)
+        each(0 if i else 1, group, lambda t: qd_arrival(block, t).wait_recv())
+        raw, aug = [], []
+        for d in range(per):
+            for g in range(F):
+                both = qd_in[block * per + d, g].astype(F32)
+                raw.append(both)
+                aug.append(jnp.where(lane < DH, both * scale, hot[g]))
+        raw = jnp.concatenate(raw, axis=0)
+        qaug[i] = jnp.concatenate(aug, axis=0).astype(BF)
+        xraw[i] = raw.astype(BF)
+        qdz[i, :QC] = jnp.where(tall < DH, raw * scale, 0.0).astype(BF)
+        qdz[i, QC:] = jnp.where(tall >= DH, raw, 0.0).astype(BF)
+
+    def forth(j, i):
+        raw = rdot(kaug[j], qaug[i])
+        top = jnp.max(raw, axis=0, keepdims=True)
+        if j:
+            old = top_ref[i]
+            top = jnp.maximum(old, top)
+        expo = jnp.exp(raw - top)
+        dprod = rdot(vz[j], xraw[i])
+        sbuf[j, i] = expo
+        dpbuf[j, i] = dprod
+        tops[j, i] = top
+        top_ref[i] = top
+        total = jnp.sum(expo, axis=0, keepdims=True)
+        dsum = jnp.sum(expo * dprod, axis=0, keepdims=True)
+        if j:
+            keep = jnp.exp(old - top)
+            total = total_ref[i] * keep + total
+            dsum = dsum_ref[i] * keep + dsum
+        total_ref[i] = total
+        dsum_ref[i] = dsum
+
+    spans = [(c, min(c + PAIR, QC)) for c in range(0, QC, PAIR)]
+
+    def st_copy(i):
+        return remote(st_send.at[i], st_in.at[block_of(i)], st_ss.at[i], st_rs.at[block_of(i)], (f, other * L + l))
+
+    def give(i):
+        for s, ref in enumerate((top_ref, total_ref, dsum_ref)):
+            value = ref[i]
+            for n, (lo, hi) in enumerate(spans):
+                at = s * len(spans) + n
+                st_send[i, at:at + 1, :hi - lo] = value[:, lo:hi]
+        st_copy(i).start()
+
+    def meet(i, block):
+        here = st_in.at[block]
+        remote(here, here, st_ss.at[0], st_rs.at[block], (f, other * L + l)).wait_recv()
+        got = []
+        for s in range(3):
+            got.append(jnp.concatenate(
+                [st_in[block, s * len(spans) + n:s * len(spans) + n + 1, :hi - lo] for n, (lo, hi) in enumerate(spans)],
+                axis=1))
+        mine = top_ref[i]
+        top = jnp.maximum(mine, got[0])
+        a, b = jnp.exp(mine - top), jnp.exp(got[0] - top)
+        inv = 1.0 / (total_ref[i] * a + got[1] * b)
+        top_ref[i] = top
+        dsum_ref[i] = (dsum_ref[i] * a + got[2] * b) * inv
+        total_ref[i] = inv
+
+    def back(j, i):
+        factor = jnp.exp(tops[j, i] - top_ref[i]) * total_ref[i]
+        prob = sbuf[j, i] * factor
+        dscore = (prob * (dpbuf[j, i] - dsum_ref[i])).astype(BF)
+        added = dot(jnp.concatenate([dscore, prob.astype(BF)], axis=1), qdz[i])
+        acc[j] += added.reshape(per, F, rows, PAIR)
+        more = dot(kt[j], dscore)
+        if j:
+            more = dqacc[...] + more
+        dqacc[...] = more
+
+    def dq_copy(i, block, t):
+        d, ff = around(t)
+        return remote(dq_send.at[i, d, ff], dq_in.at[part, head], dq_ss.at[i * group + t],
+                      dq_rs.at[part * heads + head], (ff, block * per + d))
+
+    def dq_own(i):
+        return pltpu.make_async_copy(dq_send.at[i, d0, f], dq_in.at[part, head], own_sem.at[0])
+
+    def ship_queries(i, block, slot):
+        dqs[...] = jnp.concatenate([dqacc[...], jnp.zeros((DH, QC), F32)], axis=0).T
+        for d in range(per):
+            for g in range(F):
+                base = (d * F + g) * rows
+                dq_send[i, d, g] = jnp.concatenate(
+                    [dqs[base:base + half, :DH], dqs[base + rows - half:base + rows, :DH]], axis=1).astype(BF)
+        if slot >= U:
+            dq_copy(i, block, 0).start()
+        else:
+            @pl.when(i == 0)
+            def _():
+                dq_own(i).start()
+
+            @pl.when(i != 0)
+            def _():
+                dq_copy(i, block, 0).start()
+        each(1, group, lambda t: dq_copy(i, block, t).start())
+
+    def fin_copy(t):
+        ff, ll = near(t)
+        return remote(fin_send.at[lax.div(t, group), lax.rem(ll, per), ff], fin_in.at[head], fin_ss.at[t],
+                      fin_rs.at[head], (ff, part * L + ll))
+
+    def fin_own():
+        return pltpu.make_async_copy(fin_send.at[0, d0, f], fin_in.at[head], own_sem.at[1])
+
+    def ship_keys(j):
+        fin_send[j] = acc[j].astype(BF)
+        if j == 0:
+            fin_own().start()
+        each(max(j * group, 1), (j + 1) * group, lambda t: fin_copy(t).start())
+
+    for i in range(U):
+        for j in range(U):
+            if i == 0:
+                take_keys(j)
+            if j == 0:
+                take_queries(i)
+            forth(j, i)
+        give(i)
+    for i in range(U, 2 * U):
+        take_queries(i)
+        for j in range(U):
+            forth(j, i)
+        give(i)
+        meet(i, block_of(i))
+        for j in range(U):
+            back(j, i)
+        ship_queries(i, block_of(i), i)
+    for n in range(U):
+        u = n + (1 - part) * (U - 1 - 2 * n)
+        i = lax.rem(u + U - u0, U)
+        meet(i, part * U + u)
+        for j in range(U):
+            back(j, i)
+            if n == U - 1:
+                if j == U - 1:
+                    ship_queries(i, part * U + u, n)
+                ship_keys(j)
+        if n < U - 1:
+            ship_queries(i, part * U + u, n)
+
+    def dq_arrival(t):
+        ff, ww = lax.rem(f + lax.rem(t, F), F), lax.rem(w + lax.div(t, F), W)
+        pp, hh = lax.div(ww, L), ff * L + lax.rem(ww, L)
+        here = dq_in.at[pp, hh]
+        return remote(here, here, dq_ss.at[0], dq_rs.at[pp * heads + hh], (ff, ww))
+
+    def fin_arrival(t):
+        ff, ll = near(t)
+        here = fin_in.at[ff * L + ll]
+        return remote(here, here, fin_ss.at[t], fin_rs.at[ff * L + ll], (ff, part * L + ll))
+
+    each(1, F * W, lambda t: dq_arrival(t).wait_recv())
+    each(1, heads, lambda t: fin_arrival(t).wait_recv())
+    dq_own(0).wait()
+    fin_own().wait()
+
+    def sent(t):
+        kv_copy(t).wait_send()
+        qd_copy(t).wait_send()
+        fin_copy(t).wait_send()
+
+    each(1, heads, sent)
+    each(0, heads, lambda t: qd_cross(t).wait_send())
+    for i in range(2 * U):
+        st_copy(i).wait_send()
+        each(0 if i else 1, group, lambda t: dq_copy(i, block_of(i), t).wait_send())
+
+
+def both_halves(dq_in, fin_in, dq_out, dk_out, dv_out):
+    half, rows, width = dq_in.shape[2], dq_out.shape[1], dq_out.shape[2]
+    for j in range(width // PAIR):
+        cols = slice(j * PAIR, (j + 1) * PAIR)
+        sides = []
+        for h in (2 * j, 2 * j + 1):
+            got = dq_in[0, h].astype(F32) + dq_in[1, h].astype(F32)
+            sides.append(jnp.concatenate([got[:, :DH], got[2 * half - rows:, DH:]], axis=0))
+        dq_out[0, :, cols] = jnp.concatenate(sides, axis=1).astype(BF)
+        one, two = fin_in[2 * j], fin_in[2 * j + 1]
+        dk_out[0, :, cols] = jnp.concatenate([one[:, :DH], two[:, :DH]], axis=1)
+        dv_out[0, :, cols] = jnp.concatenate([one[:, DH:], two[:, DH:]], axis=1)
+
+
+def local_halves(F, W, queries, keys_in, values_in, grad_out, partners, registers):
+    _, rows, width = queries.shape
+    heads = width // DH
+    L = W // 2
+    half = ((rows + 1) // 2 + 7) // 8 * 8
+    per = next(n for n in range(L, 0, -1) if L % n == 0 and (n == 1 or n * F * rows <= UNIT))
+    U = L // per
+    unit = per * F * rows
+    C = 2 * U
+    stats = (3 * ((unit + PAIR - 1) // PAIR) + 7) // 8 * 8
+    vm = lambda *shape: pltpu.VMEM(shape, BF)
+    vf = lambda *shape: pltpu.VMEM(shape, F32)
+    dma = lambda n: pltpu.SemaphoreType.DMA((n,))
+    out = jax.ShapeDtypeStruct((1, rows, width), BF)
+    dq_heads, kv_heads = pl.pallas_call(
+        functools.partial(halves, F, W),
+        out_shape=(jax.ShapeDtypeStruct((2, heads, half, PAIR), BF), jax.ShapeDtypeStruct((heads, rows, PAIR), BF)),
+        in_specs=[pl.BlockSpec(memory_space=pltpu.SMEM)] * 2 + [pl.BlockSpec(memory_space=pltpu.VMEM)] * 4,
+        out_specs=(pl.BlockSpec(memory_space=pl.ANY),) * 2,
+        scratch_shapes=[
+            vm(heads, rows, PAIR), vm(heads, rows, PAIR), vm(L, F, rows, PAIR), vm(W, F, rows, PAIR),
+            vm(U, unit, PAIR), vm(U, unit, PAIR), vm(U, DH, unit),
+            vm(C, unit, PAIR), vm(C, unit, PAIR), vm(C, 2 * unit, PAIR),
+            vf(U, C, unit, unit), vf(U, C, unit, unit), vf(U, per, F, rows, PAIR),
+            vf(DH, unit), vf(unit, PAIR),
+            vf(U, C, 1, unit), vf(C, 1, unit), vf(C, 1, unit), vf(C, 1, unit),
+            vf(C, stats, PAIR), vf(C, stats, PAIR),
+            vm(U, per, F, rows, PAIR), vm(C, per, F, half, PAIR), dma(2),
+            dma(heads), dma(heads), dma(2 * heads), dma(2 * heads), dma(C), dma(C),
+            dma(2 * heads), dma(2 * heads), dma(heads), dma(heads),
+        ],
+        compiler_params=pltpu.CompilerParams(
+            collective_id=0, has_side_effects=True, vmem_limit_bytes=60 * 2 ** 20),
+    )(partners.T, registers, queries, keys_in, values_in, grad_out)
+    return pl.pallas_call(
+        both_halves,
+        out_shape=(out, out, out),
+        in_specs=[pl.BlockSpec(memory_space=pltpu.VMEM)] * 2,
+        out_specs=(pl.BlockSpec(memory_space=pltpu.VMEM),) * 3,
+    )(dq_heads, kv_heads)
+
+
+def choose(F, W, queries, *others):
+    _, rows, width = queries.shape
+    heads = width // DH
+    held = 2 * F * W // 2 * rows * F * W * rows * 4
+    if W % 2 == 0 and F * W == 2 * heads and SPLITS * F <= DH and held <= 24 * 2 ** 20:
+        return local_halves(F, W, queries, *others)
+    return local(F, W, queries, *others)
+
+
 def solution(mesh):
     spec = P("frame", "within", None)
     return jax.shard_map(
-        functools.partial(local, mesh.shape["frame"], mesh.shape["within"]),
+        functools.partial(choose, mesh.shape["frame"], mesh.shape["within"]),
         mesh=mesh,
         in_specs=(spec, spec, spec, spec, P(), P()),
         out_specs=(spec, spec, spec),

time: 48.1 us -> 48.7 us (1.012)
  Pallas kernels: 47.3 us -> 47.9 us
    pallas_call x2, Pallas kernels: 47.3 us -> 47.9 us  [the longest x1 45.7 us: local_halves(): pl.pallas_call(functools.partial(halves, F, W), out_shape=(jax.ShapeDtype...]
where the time goes in v1:
time: 48.7 us; the launch traced here: 48.5 us
  Pallas kernels  47.9 us (98%)
  between operations  0.64 us (1%)
    pallas_call x1, Pallas kernels, local_halves(): pl.pallas_call(functools.partial(halves, F, W), out_shape=(jax.ShapeDtype...  45.7 us
    pallas_call x1, Pallas kernels, local_halves(): pl.pallas_call(both_halves, out_shape=(out, out, out), in_specs=[pl.Block...  2.14 us

profile of v1, /device:TPU:0, one launch (start us, length us, event | category | flops | bytes accessed | tf_op | source)
XLA Modules:
  0.0 48.5 jit_solution(14872193188117961260)
XLA Ops:
  0.6 45.7 %shard_map.85 = (bf16[2,16,40,128]{3,2,1,0:T(8,128)(2,1)}, bf16[16,72,128]{2,1,0:T(8,128)(2,1)}) custom-call(s32[2,4]{1,0:T(2,128)} %bitcast.1, s32[4]{0:T(128)} %reg_ref.1, bf16[1,72,1024]{2,1,0:T(8,128)(2,1)} %q_ref.1, bf16[1,72,1024]{2,1,0:T(8,128)(2,1)} %k_ref.1, bf16[1,72,1024]{2,1,0:T(8,128)(2,1)} %v_ref.1, bf16[1,72,1024]{2,1,0:T(8,128)(2,1)} %d_ref.1), custom_call_target="tpu_custom_call" | custom-call | tf_op jit(solution)/shard_map/pallas_call | solution.py:745
  46.4 2.1 %shard_map.86 = (bf16[1,72,1024]{2,1,0:T(8,128)(2,1)}, bf16[1,72,1024]{2,1,0:T(8,128)(2,1)}, bf16[1,72,1024]{2,1,0:T(8,128)(2,1)}) custom-call(bf16[2,16,40,128]{3,2,1,0:T(8,128)(2,1)} %get-tuple-element.5.dq_in, bf16[16,72,128]{2,1,0:T(8,128)(2,1)} %get-tuple-element.6.fin_in), custom_call_target="tpu_custom_call" | custom-call | tf_op jit(solution)/shard_map/pallas_call | solution.py:765

commit v2 on v1

--- a/solution.py
+++ b/solution.py
@@ -399,102 +399,127 @@
     )(dq_heads, kv_heads)
 
 
-def halves(F, W, part_ref, reg_ref, q_ref, k_ref, v_ref, d_ref, dq_in, fin_in,
-           kv_send, qd_send, kv_in, qd_in, kaug, vz, kt, qaug, xraw, qdz, sbuf, dpbuf, acc, dqacc, dqs,
-           tops, top_ref, total_ref, dsum_ref, st_send, st_in, fin_send, dq_send, own_sem,
-           kv_ss, kv_rs, qd_ss, qd_rs, st_ss, st_rs, dq_ss, dq_rs, fin_ss, fin_rs):
+def halves(F, W, part_hbm, reg_hbm, q_hbm, k_hbm, v_hbm, d_hbm, dq_in, fin_in,
+           part_ref, reg_ref, q_ref, k_ref, v_ref, d_ref, kv_send, qd_send, kv_in, qd_in,
+           kaug, vz, kt, qaug, xraw, qdz, sbuf, dpbuf, acc, dqacc, dqs,
+           tops, top_ref, total_ref, dsum_ref, st_send, st_in, fin_send, dq_send,
+           in_sem, kv_ss, kv_rs, qd_ss, qd_rs, st_ss, st_rs, dq_ss, dq_rs, fin_ss, fin_rs, below, above):
     rows, width = q_ref.shape[1], q_ref.shape[2]
     n_slots = part_ref.shape[0]
-    U, per = acc.shape[0], acc.shape[1]
+    U, per = kv_in.shape[0], kv_in.shape[1]
     L = U * per
+    B = 2 * U
     heads = F * L
     group = per * F
     unit = group * rows
     QC = unit
     scale = DH ** -0.5
-    half = dq_send.shape[3]
+    half = dq_send.shape[1]
     f = lax.axis_index("frame")
     w = lax.axis_index("within")
-    part = lax.div(w, L)
+    block0 = lax.div(w, per)
+    d0 = lax.rem(w, per)
+    part = lax.div(block0, U)
     other = 1 - part
-    l = lax.rem(w, L)
-    u0 = lax.div(l, per)
-    d0 = lax.rem(l, per)
+    u0 = lax.rem(block0, U)
+    l = u0 * per + d0
     head = f * L + l
 
     barrier = pltpu.get_barrier_semaphore()
 
+    def around(t):
+        return lax.rem(d0 + lax.div(t, F), per), lax.rem(f + lax.rem(t, F), F)
+
+    def knock(sem, block, d, ff):
+        pl.semaphore_signal(sem, inc=1, device_id=(ff, block * per + d), device_id_type=MESH)
+
     def greet(t):
-        pl.semaphore_signal(barrier, inc=1, device_id=(lax.rem(f + lax.rem(t, F), F), lax.rem(w + lax.div(t, F), W)),
-                            device_id_type=MESH)
-
-    each(1, F * W, greet)
+        d, ff = around(group - t)
+        knock(barrier, block0, d, ff)
+
+    @pl.when(block0 > 0)
+    def _():
+        knock(barrier, block0 - 1, d0, f)
+
+    @pl.when(block0 < B - 1)
+    def _():
+        knock(barrier, block0 + 1, d0, f)
+
+    each(1, group, greet)
+    loads = [pltpu.make_async_copy(src, dst, in_sem.at[n]) for n, (src, dst) in enumerate(
+        ((k_hbm, k_ref), (v_hbm, v_ref), (q_hbm, q_ref), (d_hbm, d_ref), (part_hbm, part_ref), (reg_hbm, reg_ref)))]
+    for load in loads:
+        load.start()
 
     for first, second, out in ((k_ref, v_ref, kv_send), (q_ref, d_ref, qd_send)):
+        for load in (loads.pop(0), loads.pop(0)):
+            load.wait()
         for j in range(width // PAIR):
             cols = slice(j * PAIR, (j + 1) * PAIR)
             one = first[0, :, cols]
             two = second[0, :, cols]
             out[2 * j] = jnp.concatenate([one[:, :DH], two[:, :DH]], axis=1)
             out[2 * j + 1] = jnp.concatenate([one[:, DH:], two[:, DH:]], axis=1)
-    kv_in[l, f] = kv_send[head]
-    qd_in[w, f] = qd_send[head]
-
-    pl.semaphore_wait(barrier, F * W - 1)
-
-    def around(t):
-        return lax.rem(d0 + lax.div(lax.rem(t, group), F), per), lax.rem(f + lax.rem(t, F), F)
-
-    def near(t):
-        d, ff = around(t)
-        return ff, lax.rem(u0 + lax.div(t, group), U) * per + d
-
-    def far(t):
-        d, ff = around(lax.div(t, U))
-        return ff, lax.rem(u0 + lax.rem(t, U), U) * per + d
 
     def remote(src, dst, ss, rs, device):
         return pltpu.make_async_remote_copy(src_ref=src, dst_ref=dst, send_sem=ss, recv_sem=rs,
                                             device_id=device, device_id_type=MESH)
 
-    def kv_copy(t):
-        ff, ll = near(t)
-        return remote(kv_send.at[ff * L + ll], kv_in.at[l, f], kv_ss.at[t], kv_rs.at[l * F + f], (ff, part * L + ll))
-
-    def kv_arrival(t):
-        ff, ll = near(t)
-        here = kv_in.at[ll, ff]
-        return remote(here, here, kv_ss.at[t], kv_rs.at[ll * F + ff], (ff, part * L + ll))
-
-    def qd_copy(t):
-        ff, ll = near(t)
-        return remote(qd_send.at[ff * L + ll], qd_in.at[w, f], qd_ss.at[t], qd_rs.at[w * F + f], (ff, part * L + ll))
-
-    def qd_cross(t):
-        ff, ll = far(t)
-        return remote(qd_send.at[ff * L + ll], qd_in.at[w, f], qd_ss.at[heads + t], qd_rs.at[w * F + f],
-                      (ff, other * L + ll))
-
-    def block_of(slot):
-        if slot < U:
-            return part * U + lax.rem(u0 + slot, U)
-        return other * U + (slot - U) + part * (U - 1 - 2 * (slot - U))
-
-    def qd_arrival(block, t):
+    def head_at(block, d, ff):
+        return ff * L + lax.rem(block, U) * per + d
+
+    def kv_copy(block, t):
         d, ff = around(t)
-        ww = block * per + d
-        here = qd_in.at[ww, ff]
-        return remote(here, here, qd_ss.at[t], qd_rs.at[ww * F + ff], (ff, ww))
-
-    def send_near(t):
-        kv_copy(t).start()
-        qd_copy(t).start()
-
-    each(1, heads, send_near)
-    each(0, heads, lambda t: qd_cross(t).start())
+        return remote(kv_send.at[head_at(block, d, ff)], kv_in.at[u0, d0, f], kv_ss.at[0], kv_rs.at[u0],
+                      (ff, block * per + d))
+
+    def qd_copy(block, t):
+        d, ff = around(t)
+        return remote(qd_send.at[head_at(block, d, ff)], qd_in.at[block0, d0, f], qd_ss.at[0], qd_rs.at[block0],
+                      (ff, block * per + d))
+
+    def send_block(block, first):
+        @pl.when(lax.div(block, U) == part)
+        def _():
+            each(first, group, lambda t: kv_copy(block, t).start())
+        each(first, group, lambda t: qd_copy(block, t).start())
+
+    pltpu.make_async_copy(kv_send.at[head], kv_in.at[u0, d0, f], kv_rs.at[u0]).start()
+    pltpu.make_async_copy(qd_send.at[head], qd_in.at[block0, d0, f], qd_rs.at[block0]).start()
+    pl.semaphore_wait(barrier, group - 1 + jnp.where(block0 > 0, 1, 0) + jnp.where(block0 < B - 1, 1, 0))
+
+    @pl.when(block0 > 0)
+    def _():
+        knock(above, block0 - 1, d0, f)
+
+    @pl.when(block0 < B - 1)
+    def _():
+        knock(below, block0 + 1, d0, f)
+
+    send_block(block0, 1)
+    for n in range(1, B):
+        @pl.when(block0 >= n)
+        def _():
+            pl.semaphore_wait(below, 1)
+
+            @pl.when(block0 < B - 1)
+            def _():
+                knock(below, block0 + 1, d0, f)
+            send_block(block0 - n, 0)
+
+        @pl.when(block0 + n < B)
+        def _():
+            pl.semaphore_wait(above, 1)
+
+            @pl.when(block0 > 0)
+            def _():
+                knock(above, block0 - 1, d0, f)
+            send_block(block0 + n, 0)
 
     acc[...] = jnp.zeros_like(acc)
     st_send[...] = jnp.zeros_like(st_send)
+    for load in loads:
+        load.wait()
 
     lane1 = lax.broadcasted_iota(jnp.int32, (1, PAIR), 1)
     table = [pieces_of(HIDDEN)] + [pieces_of(math.log(n)) for n in range(1, n_slots + 2)]
@@ -517,15 +542,18 @@
     lane = lax.broadcasted_iota(jnp.int32, (rows, PAIR), 1)
     row = lax.broadcasted_iota(jnp.int32, (rows, PAIR), 0)
     tall = lax.broadcasted_iota(jnp.int32, (unit, PAIR), 1)
-
-    def prepare(j):
+    hot = [jnp.where((lane >= DH + SPLITS * g) & (lane < DH + SPLITS * (g + 1)), 1.0, 0.0) for g in range(F)]
+
+    def take_keys(j):
         u = lax.rem(u0 + j, U)
+        here = kv_in.at[u]
+        remote(here, here, kv_ss.at[0], kv_rs.at[u], (f, w)).wait_recv()
         aug, raw = [], []
         for d in range(per):
-            ll = u * per + d
+            first = ((part * U + u) * per + d) * rows
             for p in range(F):
-                both = kv_in[ll, p].astype(F32)
-                extra = jnp.where(row + (part * L + ll) * rows >= reg_ref[p], marks[p][0], marks[p][1])
+                both = kv_in[u, d, p].astype(F32)
+                extra = jnp.where(row + first >= reg_ref[p], marks[p][0], marks[p][1])
                 raw.append(both)
                 aug.append(jnp.where(lane < DH, both, extra))
         raw = jnp.concatenate(raw, axis=0)
@@ -533,19 +561,13 @@
         vz[j] = jnp.where(tall >= DH, raw, 0.0).astype(BF)
         kt[j] = (raw * scale).T[:DH].astype(BF)
 
-    def take_keys(j):
-        each(max(j * group, 1), (j + 1) * group, lambda t: kv_arrival(t).wait_recv())
-        prepare(j)
-
-    hot = [jnp.where((lane >= DH + SPLITS * g) & (lane < DH + SPLITS * (g + 1)), 1.0, 0.0) for g in range(F)]
-
     def take_queries(i):
-        block = block_of(i)
-        each(0 if i else 1, group, lambda t: qd_arrival(block, t).wait_recv())
+        here = qd_in.at[i]
+        remote(here, here, qd_ss.at[0], qd_rs.at[i], (f, w)).wait_recv()
         raw, aug = [], []
         for d in range(per):
             for g in range(F):
-                both = qd_in[block * per + d, g].astype(F32)
+                both = qd_in[i, d, g].astype(F32)
                 raw.append(both)
                 aug.append(jnp.where(lane < DH, both * scale, hot[g]))
         raw = jnp.concatenate(raw, axis=0)
@@ -577,24 +599,21 @@
 
     spans = [(c, min(c + PAIR, QC)) for c in range(0, QC, PAIR)]
 
-    def st_copy(i):
-        return remote(st_send.at[i], st_in.at[block_of(i)], st_ss.at[i], st_rs.at[block_of(i)], (f, other * L + l))
-
     def give(i):
         for s, ref in enumerate((top_ref, total_ref, dsum_ref)):
             value = ref[i]
             for n, (lo, hi) in enumerate(spans):
                 at = s * len(spans) + n
                 st_send[i, at:at + 1, :hi - lo] = value[:, lo:hi]
-        st_copy(i).start()
-
-    def meet(i, block):
-        here = st_in.at[block]
-        remote(here, here, st_ss.at[0], st_rs.at[block], (f, other * L + l)).wait_recv()
+        remote(st_send.at[i], st_in.at[i], st_ss.at[0], st_rs.at[i], (f, other * L + l)).start()
+
+    def meet(i):
+        here = st_in.at[i]
+        remote(here, here, st_ss.at[0], st_rs.at[i], (f, other * L + l)).wait_recv()
         got = []
         for s in range(3):
             got.append(jnp.concatenate(
-                [st_in[block, s * len(spans) + n:s * len(spans) + n + 1, :hi - lo] for n, (lo, hi) in enumerate(spans)],
+                [st_in[i, s * len(spans) + n:s * len(spans) + n + 1, :hi - lo] for n, (lo, hi) in enumerate(spans)],
                 axis=1))
         mine = top_ref[i]
         top = jnp.maximum(mine, got[0])
@@ -609,109 +628,98 @@
         prob = sbuf[j, i] * factor
         dscore = (prob * (dpbuf[j, i] - dsum_ref[i])).astype(BF)
         added = dot(jnp.concatenate([dscore, prob.astype(BF)], axis=1), qdz[i])
-        acc[j] += added.reshape(per, F, rows, PAIR)
+        acc[j] += added.reshape(group, rows, PAIR)
         more = dot(kt[j], dscore)
         if j:
             more = dqacc[...] + more
         dqacc[...] = more
 
-    def dq_copy(i, block, t):
+    def dq_copy(i, t):
         d, ff = around(t)
-        return remote(dq_send.at[i, d, ff], dq_in.at[part, head], dq_ss.at[i * group + t],
-                      dq_rs.at[part * heads + head], (ff, block * per + d))
-
-    def dq_own(i):
-        return pltpu.make_async_copy(dq_send.at[i, d0, f], dq_in.at[part, head], own_sem.at[0])
-
-    def ship_queries(i, block, slot):
+        return remote(dq_send.at[i * group + d * F + ff], dq_in.at[part, head], dq_ss.at[0], dq_rs.at[part], (ff, i * per + d))
+
+    def ship_queries(i):
         dqs[...] = jnp.concatenate([dqacc[...], jnp.zeros((DH, QC), F32)], axis=0).T
         for d in range(per):
             for g in range(F):
                 base = (d * F + g) * rows
-                dq_send[i, d, g] = jnp.concatenate(
+                dq_send[i * group + d * F + g] = jnp.concatenate(
                     [dqs[base:base + half, :DH], dqs[base + rows - half:base + rows, :DH]], axis=1).astype(BF)
-        if slot >= U:
-            dq_copy(i, block, 0).start()
-        else:
-            @pl.when(i == 0)
-            def _():
-                dq_own(i).start()
-
-            @pl.when(i != 0)
-            def _():
-                dq_copy(i, block, 0).start()
-        each(1, group, lambda t: dq_copy(i, block, t).start())
-
-    def fin_copy(t):
-        ff, ll = near(t)
-        return remote(fin_send.at[lax.div(t, group), lax.rem(ll, per), ff], fin_in.at[head], fin_ss.at[t],
-                      fin_rs.at[head], (ff, part * L + ll))
-
-    def fin_own():
-        return pltpu.make_async_copy(fin_send.at[0, d0, f], fin_in.at[head], own_sem.at[1])
+
+        @pl.when(i == block0)
+        def _():
+            pltpu.make_async_copy(dq_send.at[i * group + d0 * F + f], dq_in.at[part, head], dq_rs.at[part]).start()
+
+        @pl.when(i != block0)
+        def _():
+            dq_copy(i, 0).start()
+        each(1, group, lambda t: dq_copy(i, t).start())
+
+    def fin_copy(j, t):
+        d, ff = around(t)
+        return remote(fin_send.at[j * group + d * F + ff], fin_in.at[head], fin_ss.at[0], fin_rs.at[0],
+                      (ff, (part * U + lax.rem(u0 + j, U)) * per + d))
 
     def ship_keys(j):
-        fin_send[j] = acc[j].astype(BF)
+        fin_send[j * group:(j + 1) * group] = acc[j].astype(BF)
         if j == 0:
-            fin_own().start()
-        each(max(j * group, 1), (j + 1) * group, lambda t: fin_copy(t).start())
-
-    for i in range(U):
+            pltpu.make_async_copy(fin_send.at[d0 * F + f], fin_in.at[head], fin_rs.at[0]).start()
+        each(0 if j else 1, group, lambda t: fin_copy(j, t).start())
+
+    def local(n):
+        return part * U + lax.rem(u0 + n, U)
+
+    def remote_block(n):
+        return other * U + n + part * (U - 1 - 2 * n)
+
+    edge = jnp.where(part == 0, U - 1, 0) == u0
+    order = [local(0)]
+    for n in range(U - 1):
+        order.append(jnp.where(edge, remote_block(n), local(n + 1)))
+        order.append(jnp.where(edge, local(n + 1), remote_block(n)))
+    order.append(remote_block(U - 1))
+
+    for n, i in enumerate(order):
+        if n == B - 1:
+            for e in range(U - 1):
+                meet(remote_block(e))
+                for j in range(U):
+                    back(j, remote_block(e))
+                ship_queries(remote_block(e))
+        if n:
+            take_queries(i)
         for j in range(U):
-            if i == 0:
+            if n == 0:
                 take_keys(j)
-            if j == 0:
-                take_queries(i)
+                if j == 0:
+                    take_queries(i)
             forth(j, i)
         give(i)
-    for i in range(U, 2 * U):
-        take_queries(i)
-        for j in range(U):
-            forth(j, i)
-        give(i)
-        meet(i, block_of(i))
+    last = [remote_block(U - 1)] + [part * U + n + other * (U - 1 - 2 * n) for n in range(U)]
+    for n, i in enumerate(last):
+        meet(i)
         for j in range(U):
             back(j, i)
-        ship_queries(i, block_of(i), i)
-    for n in range(U):
-        u = n + (1 - part) * (U - 1 - 2 * n)
-        i = lax.rem(u + U - u0, U)
-        meet(i, part * U + u)
-        for j in range(U):
-            back(j, i)
-            if n == U - 1:
-                if j == U - 1:
-                    ship_queries(i, part * U + u, n)
+            if n == U and j == U - 1:
+                ship_queries(i)
+            if n == U:
                 ship_keys(j)
-        if n < U - 1:
-            ship_queries(i, part * U + u, n)
-
-    def dq_arrival(t):
-        ff, ww = lax.rem(f + lax.rem(t, F), F), lax.rem(w + lax.div(t, F), W)
-        pp, hh = lax.div(ww, L), ff * L + lax.rem(ww, L)
-        here = dq_in.at[pp, hh]
-        return remote(here, here, dq_ss.at[0], dq_rs.at[pp * heads + hh], (ff, ww))
-
-    def fin_arrival(t):
-        ff, ll = near(t)
-        here = fin_in.at[ff * L + ll]
-        return remote(here, here, fin_ss.at[t], fin_rs.at[ff * L + ll], (ff, part * L + ll))
-
-    each(1, F * W, lambda t: dq_arrival(t).wait_recv())
-    each(1, heads, lambda t: fin_arrival(t).wait_recv())
-    dq_own(0).wait()
-    fin_own().wait()
-
-    def sent(t):
-        kv_copy(t).wait_send()
-        qd_copy(t).wait_send()
-        fin_copy(t).wait_send()
-
-    each(1, heads, sent)
-    each(0, heads, lambda t: qd_cross(t).wait_send())
-    for i in range(2 * U):
-        st_copy(i).wait_send()
-        each(0 if i else 1, group, lambda t: dq_copy(i, block_of(i), t).wait_send())
+        if n < U:
+            ship_queries(i)
+
+    def sent(ref, sem):
+        remote(ref, ref, sem.at[0], sem.at[0], (f, w)).wait_send()
+
+    sent(kv_send.at[pl.ds(0, heads - 1)], kv_ss)
+    sent(qd_send, qd_ss)
+    sent(qd_send.at[pl.ds(0, heads - 1)], qd_ss)
+    sent(st_send, st_ss)
+    for side in (other, part):
+        here = dq_in.at[side]
+        remote(here, here, dq_ss.at[0], dq_rs.at[side], (f, w)).wait_recv()
+    remote(fin_in, fin_in, fin_ss.at[0], fin_rs.at[0], (f, w)).wait_recv()
+    sent(dq_send.at[pl.ds(0, B * group - 1)], dq_ss)
+    sent(fin_send.at[pl.ds(0, U * group - 1)], fin_ss)
 
 
 def both_halves(dq_in, fin_in, dq_out, dk_out, dv_out):
@@ -745,19 +753,21 @@
     dq_heads, kv_heads = pl.pallas_call(
         functools.partial(halves, F, W),
         out_shape=(jax.ShapeDtypeStruct((2, heads, half, PAIR), BF), jax.ShapeDtypeStruct((heads, rows, PAIR), BF)),
-        in_specs=[pl.BlockSpec(memory_space=pltpu.SMEM)] * 2 + [pl.BlockSpec(memory_space=pltpu.VMEM)] * 4,
+        in_specs=[pl.BlockSpec(memory_space=pl.ANY)] * 6,
         out_specs=(pl.BlockSpec(memory_space=pl.ANY),) * 2,
         scratch_shapes=[
-            vm(heads, rows, PAIR), vm(heads, rows, PAIR), vm(L, F, rows, PAIR), vm(W, F, rows, PAIR),
+            pltpu.SMEM(partners.T.shape, jnp.int32), pltpu.SMEM(registers.shape, jnp.int32),
+            vm(1, rows, width), vm(1, rows, width), vm(1, rows, width), vm(1, rows, width),
+            vm(heads, rows, PAIR), vm(heads, rows, PAIR), vm(U, per, F, rows, PAIR), vm(C, per, F, rows, PAIR),
             vm(U, unit, PAIR), vm(U, unit, PAIR), vm(U, DH, unit),
             vm(C, unit, PAIR), vm(C, unit, PAIR), vm(C, 2 * unit, PAIR),
-            vf(U, C, unit, unit), vf(U, C, unit, unit), vf(U, per, F, rows, PAIR),
+            vf(U, C, unit, unit), vf(U, C, unit, unit), vf(U, per * F, rows, PAIR),
             vf(DH, unit), vf(unit, PAIR),
             vf(U, C, 1, unit), vf(C, 1, unit), vf(C, 1, unit), vf(C, 1, unit),
             vf(C, stats, PAIR), vf(C, stats, PAIR),
-            vm(U, per, F, rows, PAIR), vm(C, per, F, half, PAIR), dma(2),
-            dma(heads), dma(heads), dma(2 * heads), dma(2 * heads), dma(C), dma(C),
-            dma(2 * heads), dma(2 * heads), dma(heads), dma(heads),
+            vm(heads, rows, PAIR), vm(C * per * F, half, PAIR),
+            dma(6), dma(1), dma(U), dma(1), dma(C), dma(1), dma(C), dma(1), dma(2), dma(1), dma(1),
+            pltpu.SemaphoreType.REGULAR, pltpu.SemaphoreType.REGULAR,
         ],
         compiler_params=pltpu.CompilerParams(
             collective_id=0, has_side_effects=True, vmem_limit_bytes=60 * 2 ** 20),

time: 48.7 us -> 41.8 us (0.86)
  Pallas kernels: 47.9 us -> 41 us
    pallas_call x1, Pallas kernels: 45.7 us -> 38.9 us  [local_halves(): pl.pallas_call(functools.partial(halves, F, W), out_shape=(jax.ShapeDtype...]
where the time goes in v2:
time: 41.8 us; the launch traced here: 41.7 us
  Pallas kernels  41 us (98%)
  between operations  0.64 us (2%)
    pallas_call x1, Pallas kernels, local_halves(): pl.pallas_call(functools.partial(halves, F, W), out_shape=(jax.ShapeDtype...  38.9 us
    pallas_call x1, Pallas kernels, local_halves(): pl.pallas_call(both_halves, out_shape=(out, out, out), in_specs=[pl.Block...  2.14 us

profile of v2, /device:TPU:0, one launch (start us, length us, event | category | flops | bytes accessed | tf_op | source)
XLA Modules:
  0.0 41.7 jit_solution(10639403332252713792)
XLA Ops:
  0.6 38.9 %shard_map.85 = (bf16[2,16,40,128]{3,2,1,0:T(8,128)(2,1)}, bf16[16,72,128]{2,1,0:T(8,128)(2,1)}) custom-call(s32[2,4]{1,0:T(2,128)} %bitcast.1, s32[4]{0:T(128)} %reg_hbm.1, bf16[1,72,1024]{2,1,0:T(8,128)(2,1)} %q_hbm.1, bf16[1,72,1024]{2,1,0:T(8,128)(2,1)} %k_hbm.1, bf16[1,72,1024]{2,1,0:T(8,128)(2,1)} %v_hbm.1, bf16[1,72,1024]{2,1,0:T(8,128)(2,1)} %d_hbm.1), custom_call_target="tpu_custom_call" | custom-call | tf_op jit(solution)/shard_map/pallas_call | solution.py:753
  39.6 2.1 %shard_map.86 = (bf16[1,72,1024]{2,1,0:T(8,128)(2,1)}, bf16[1,72,1024]{2,1,0:T(8,128)(2,1)}, bf16[1,72,1024]{2,1,0:T(8,128)(2,1)}) custom-call(bf16[2,16,40,128]{3,2,1,0:T(8,128)(2,1)} %get-tuple-element.5.dq_in, bf16[16,72,128]{2,1,0:T(8,128)(2,1)} %get-tuple-element.6.fin_in), custom_call_target="tpu_custom_call" | custom-call | tf_op jit(solution)/shard_map/pallas_call | solution.py:775

commit v3 on v2

--- a/solution.py
+++ b/solution.py
@@ -13,6 +13,8 @@
 PAIR = 2 * DH
 SPLITS = 3
 UNIT = 640
+TILE = 256
+SUB = 96
 HIDDEN = -1e30
 BF = jnp.bfloat16
 F32 = jnp.float32
@@ -412,7 +414,10 @@
     heads = F * L
     group = per * F
     unit = group * rows
-    QC = unit
+    QP = qaug.shape[1]
+    tiles = [(c, min(c + TILE, QP)) for c in range(0, QP, TILE)]
+    n_subs = tops.shape[2]
+    sub = unit // n_subs
     scale = DH ** -0.5
     half = dq_send.shape[1]
     f = lax.axis_index("frame")
@@ -518,6 +523,9 @@
 
     acc[...] = jnp.zeros_like(acc)
     st_send[...] = jnp.zeros_like(st_send)
+    if QP > unit:
+        for ref, first in ((qaug, unit), (xraw, unit), (qdz, unit), (qdz, QP + unit)):
+            ref[:, first:first + QP - unit] = jnp.zeros((B, QP - unit, PAIR), BF)
     for load in loads:
         load.wait()
 
@@ -571,66 +579,80 @@
                 raw.append(both)
                 aug.append(jnp.where(lane < DH, both * scale, hot[g]))
         raw = jnp.concatenate(raw, axis=0)
-        qaug[i] = jnp.concatenate(aug, axis=0).astype(BF)
-        xraw[i] = raw.astype(BF)
-        qdz[i, :QC] = jnp.where(tall < DH, raw * scale, 0.0).astype(BF)
-        qdz[i, QC:] = jnp.where(tall >= DH, raw, 0.0).astype(BF)
+        qaug[i, :unit] = jnp.concatenate(aug, axis=0).astype(BF)
+        xraw[i, :unit] = raw.astype(BF)
+        qdz[i, :unit] = jnp.where(tall < DH, raw * scale, 0.0).astype(BF)
+        qdz[i, QP:QP + unit] = jnp.where(tall >= DH, raw, 0.0).astype(BF)
 
     def forth(j, i):
-        raw = rdot(kaug[j], qaug[i])
-        top = jnp.max(raw, axis=0, keepdims=True)
-        if j:
-            old = top_ref[i]
-            top = jnp.maximum(old, top)
-        expo = jnp.exp(raw - top)
-        dprod = rdot(vz[j], xraw[i])
-        sbuf[j, i] = expo
-        dpbuf[j, i] = dprod
-        tops[j, i] = top
-        top_ref[i] = top
-        total = jnp.sum(expo, axis=0, keepdims=True)
-        dsum = jnp.sum(expo * dprod, axis=0, keepdims=True)
-        if j:
-            keep = jnp.exp(old - top)
-            total = total_ref[i] * keep + total
-            dsum = dsum_ref[i] * keep + dsum
-        total_ref[i] = total
-        dsum_ref[i] = dsum
-
-    spans = [(c, min(c + PAIR, QC)) for c in range(0, QC, PAIR)]
+        for lo, hi in tiles:
+            raw = rdot(kaug[j], qaug[i, lo:hi])
+            dprod = rdot(vz[j], xraw[i, lo:hi])
+            if j:
+                top, total, dsum = top_ref[i, :, lo:hi], total_ref[i, :, lo:hi], dsum_ref[i, :, lo:hi]
+            for s in range(n_subs):
+                at = slice(s * sub, (s + 1) * sub)
+                part_raw = raw[at].reshape(sub // 8, 8, hi - lo)
+                part_dp = dprod[at].reshape(sub // 8, 8, hi - lo)
+                peak = jnp.max(part_raw, axis=0)
+                if j or s:
+                    peak = jnp.maximum(top, peak)
+                expo = jnp.exp(part_raw - peak[None])
+                more, dmore = jnp.sum(expo, axis=0), jnp.sum(expo * part_dp, axis=0)
+                if j or s:
+                    keep = jnp.exp(top - peak)
+                    more, dmore = total * keep + more, dsum * keep + dmore
+                top, total, dsum = peak, more, dmore
+                sbuf[j, i, at, lo:hi] = expo.reshape(sub, hi - lo)
+                dpbuf[j, i, at, lo:hi] = part_dp.reshape(sub, hi - lo)
+                tops[j, i, s, :, lo:hi] = peak
+            top_ref[i, :, lo:hi] = top
+            total_ref[i, :, lo:hi] = total
+            dsum_ref[i, :, lo:hi] = dsum
+
+    spans = [(c, c + PAIR) for c in range(0, QP, PAIR)]
 
     def give(i):
-        for s, ref in enumerate((top_ref, total_ref, dsum_ref)):
-            value = ref[i]
+        peak = jnp.max(top_ref[i], axis=0, keepdims=True)
+        keep = jnp.exp(top_ref[i] - peak)
+        total = jnp.sum(total_ref[i] * keep, axis=0, keepdims=True)
+        dsum = jnp.sum(dsum_ref[i] * keep, axis=0, keepdims=True)
+        for s, value in enumerate((peak, total, dsum)):
             for n, (lo, hi) in enumerate(spans):
                 at = s * len(spans) + n
-                st_send[i, at:at + 1, :hi - lo] = value[:, lo:hi]
+                st_send[i, at:at + 1] = value[:, lo:hi]
         remote(st_send.at[i], st_in.at[i], st_ss.at[0], st_rs.at[i], (f, other * L + l)).start()
 
     def meet(i):
         here = st_in.at[i]
         remote(here, here, st_ss.at[0], st_rs.at[i], (f, other * L + l)).wait_recv()
-        got = []
-        for s in range(3):
-            got.append(jnp.concatenate(
-                [st_in[i, s * len(spans) + n:s * len(spans) + n + 1, :hi - lo] for n, (lo, hi) in enumerate(spans)],
-                axis=1))
-        mine = top_ref[i]
-        top = jnp.maximum(mine, got[0])
-        a, b = jnp.exp(mine - top), jnp.exp(got[0] - top)
-        inv = 1.0 / (total_ref[i] * a + got[1] * b)
-        top_ref[i] = top
-        dsum_ref[i] = (dsum_ref[i] * a + got[2] * b) * inv
-        total_ref[i] = inv
+        def row_of(ref, s):
+            return jnp.concatenate(
+                [ref[i, s * len(spans) + n:s * len(spans) + n + 1] for n in range(len(spans))], axis=1)
+
+        mine, yours = [[row_of(ref, s) for s in range(3)] for ref in (st_send, st_in)]
+        peak = jnp.maximum(mine[0], yours[0])
+        a, b = jnp.exp(mine[0] - peak), jnp.exp(yours[0] - peak)
+        inv = 1.0 / (mine[1] * a + yours[1] * b)
+        whole = (8, QP)
+        top_ref[i] = jnp.broadcast_to(peak, whole)
+        total_ref[i] = jnp.broadcast_to(inv, whole)
+        dsum_ref[i] = jnp.broadcast_to((mine[2] * a + yours[2] * b) * inv, whole)
 
     def back(j, i):
-        factor = jnp.exp(tops[j, i] - top_ref[i]) * total_ref[i]
-        prob = sbuf[j, i] * factor
-        dscore = (prob * (dpbuf[j, i] - dsum_ref[i])).astype(BF)
-        added = dot(jnp.concatenate([dscore, prob.astype(BF)], axis=1), qdz[i])
+        probs, dscores = [], []
+        for s in range(n_subs):
+            at = slice(s * sub, (s + 1) * sub)
+            factor = jnp.exp(tops[j, i, s] - top_ref[i]) * total_ref[i]
+            prob = sbuf[j, i, at].reshape(sub // 8, 8, QP) * factor[None]
+            dscore = prob * (dpbuf[j, i, at].reshape(sub // 8, 8, QP) - dsum_ref[i][None])
+            probs.append(prob.reshape(sub, QP).astype(BF))
+            dscores.append(dscore.reshape(sub, QP).astype(BF))
+        dscore = jnp.concatenate(dscores, axis=0)
+        added = dot(jnp.concatenate([dscore, jnp.concatenate(probs, axis=0)], axis=1), qdz[i])
         acc[j] += added.reshape(group, rows, PAIR)
         more = dot(kt[j], dscore)
-        if j:
+        if j < U - 1:
             more = dqacc[...] + more
         dqacc[...] = more
 
@@ -639,7 +661,7 @@
         return remote(dq_send.at[i * group + d * F + ff], dq_in.at[part, head], dq_ss.at[0], dq_rs.at[part], (ff, i * per + d))
 
     def ship_queries(i):
-        dqs[...] = jnp.concatenate([dqacc[...], jnp.zeros((DH, QC), F32)], axis=0).T
+        dqs[...] = jnp.concatenate([dqacc[...], jnp.zeros((DH, QP), F32)], axis=0).T
         for d in range(per):
             for g in range(F):
                 base = (d * F + g) * rows
@@ -680,12 +702,6 @@
     order.append(remote_block(U - 1))
 
     for n, i in enumerate(order):
-        if n == B - 1:
-            for e in range(U - 1):
-                meet(remote_block(e))
-                for j in range(U):
-                    back(j, remote_block(e))
-                ship_queries(remote_block(e))
         if n:
             take_queries(i)
         for j in range(U):
@@ -695,17 +711,15 @@
                     take_queries(i)
             forth(j, i)
         give(i)
-    last = [remote_block(U - 1)] + [part * U + n + other * (U - 1 - 2 * n) for n in range(U)]
+    last = [remote_block(n) for n in range(U)] + [local(n) for n in reversed(range(U))]
     for n, i in enumerate(last):
         meet(i)
-        for j in range(U):
+        for j in reversed(range(U)):
             back(j, i)
-            if n == U and j == U - 1:
-                ship_queries(i)
-            if n == U:
+            if n == B - 1 and j:
                 ship_keys(j)
-        if n < U:
-            ship_queries(i)
+        ship_queries(i)
+    ship_keys(0)
 
     def sent(ref, sem):
         remote(ref, ref, sem.at[0], sem.at[0], (f, w)).wait_send()
@@ -745,7 +759,9 @@
     U = L // per
     unit = per * F * rows
     C = 2 * U
-    stats = (3 * ((unit + PAIR - 1) // PAIR) + 7) // 8 * 8
+    QP = (unit + PAIR - 1) // PAIR * PAIR
+    subs = unit // next(n for n in range(SUB, 0, -8) if unit % n == 0)
+    stats = (3 * (QP // PAIR) + 7) // 8 * 8
     vm = lambda *shape: pltpu.VMEM(shape, BF)
     vf = lambda *shape: pltpu.VMEM(shape, F32)
     dma = lambda n: pltpu.SemaphoreType.DMA((n,))
@@ -760,10 +776,10 @@
             vm(1, rows, width), vm(1, rows, width), vm(1, rows, width), vm(1, rows, width),
             vm(heads, rows, PAIR), vm(heads, rows, PAIR), vm(U, per, F, rows, PAIR), vm(C, per, F, rows, PAIR),
             vm(U, unit, PAIR), vm(U, unit, PAIR), vm(U, DH, unit),
-            vm(C, unit, PAIR), vm(C, unit, PAIR), vm(C, 2 * unit, PAIR),
-            vf(U, C, unit, unit), vf(U, C, unit, unit), vf(U, per * F, rows, PAIR),
-            vf(DH, unit), vf(unit, PAIR),
-            vf(U, C, 1, unit), vf(C, 1, unit), vf(C, 1, unit), vf(C, 1, unit),
+            vm(C, QP, PAIR), vm(C, QP, PAIR), vm(C, 2 * QP, PAIR),
+            vf(U, C, unit, QP), vf(U, C, unit, QP), vf(U, per * F, rows, PAIR),
+            vf(DH, QP), vf(QP, PAIR),
+            vf(U, C, subs, 8, QP), vf(C, 8, QP), vf(C, 8, QP), vf(C, 8, QP),
             vf(C, stats, PAIR), vf(C, stats, PAIR),
             vm(heads, rows, PAIR), vm(C * per * F, half, PAIR),
             dma(6), dma(1), dma(U), dma(1), dma(C), dma(1), dma(C), dma(1), dma(2), dma(1), dma(1),

time: 41.8 us -> 41 us (0.981)
  Pallas kernels: 41 us -> 40.2 us
    pallas_call x1, Pallas kernels: 38.9 us -> 38 us  [local_halves(): pl.pallas_call(functools.partial(halves, F, W), out_shape=(jax.ShapeDtype...]
where the time goes in v3:
time: 41 us; the launch traced here: 40.8 us
  Pallas kernels  40.2 us (98%)
  between operations  0.64 us (2%)
    pallas_call x1, Pallas kernels, local_halves(): pl.pallas_call(functools.partial(halves, F, W), out_shape=(jax.ShapeDtype...  38 us
    pallas_call x1, Pallas kernels, local_halves(): pl.pallas_call(both_halves, out_shape=(out, out, out), in_specs=[pl.Block...  2.14 us

profile of v3, /device:TPU:0, one launch (start us, length us, event | category | flops | bytes accessed | tf_op | source)
XLA Modules:
  0.0 40.8 jit_solution(18261345432250746947)
XLA Ops:
  0.6 38.0 %shard_map.85 = (bf16[2,16,40,128]{3,2,1,0:T(8,128)(2,1)}, bf16[16,72,128]{2,1,0:T(8,128)(2,1)}) custom-call(s32[2,4]{1,0:T(2,128)} %bitcast.1, s32[4]{0:T(128)} %reg_hbm.1, bf16[1,72,1024]{2,1,0:T(8,128)(2,1)} %q_hbm.1, bf16[1,72,1024]{2,1,0:T(8,128)(2,1)} %k_hbm.1, bf16[1,72,1024]{2,1,0:T(8,128)(2,1)} %v_hbm.1, bf16[1,72,1024]{2,1,0:T(8,128)(2,1)} %d_hbm.1), custom_call_target="tpu_custom_call" | custom-call | tf_op jit(solution)/shard_map/pallas_call | solution.py:769
  38.7 2.1 %shard_map.86 = (bf16[1,72,1024]{2,1,0:T(8,128)(2,1)}, bf16[1,72,1024]{2,1,0:T(8,128)(2,1)}, bf16[1,72,1024]{2,1,0:T(8,128)(2,1)}) custom-call(bf16[2,16,40,128]{3,2,1,0:T(8,128)(2,1)} %get-tuple-element.5.dq_in, bf16[16,72,128]{2,1,0:T(8,128)(2,1)} %get-tuple-element.6.fin_in), custom_call_target="tpu_custom_call" | custom-call | tf_op jit(solution)/shard_map/pallas_call | solution.py:791

commit v4 on v3

--- a/solution.py
+++ b/solution.py
@@ -418,6 +418,7 @@
     tiles = [(c, min(c + TILE, QP)) for c in range(0, QP, TILE)]
     n_subs = tops.shape[2]
     sub = unit // n_subs
+    cuts = 2 if n_subs % 2 == 0 and group % 2 == 0 else 1
     scale = DH ** -0.5
     half = dq_send.shape[1]
     f = lax.axis_index("frame")
@@ -524,7 +525,8 @@
     acc[...] = jnp.zeros_like(acc)
     st_send[...] = jnp.zeros_like(st_send)
     if QP > unit:
-        for ref, first in ((qaug, unit), (xraw, unit), (qdz, unit), (qdz, QP + unit)):
+        lo, hi = tiles[-1]
+        for ref, first in ((qaug, unit), (xraw, unit), (qdz, lo + unit), (qdz, hi + unit)):
             ref[:, first:first + QP - unit] = jnp.zeros((B, QP - unit, PAIR), BF)
     for load in loads:
         load.wait()
@@ -581,8 +583,10 @@
         raw = jnp.concatenate(raw, axis=0)
         qaug[i, :unit] = jnp.concatenate(aug, axis=0).astype(BF)
         xraw[i, :unit] = raw.astype(BF)
-        qdz[i, :unit] = jnp.where(tall < DH, raw * scale, 0.0).astype(BF)
-        qdz[i, QP:QP + unit] = jnp.where(tall >= DH, raw, 0.0).astype(BF)
+        for value, side in ((jnp.where(tall < DH, raw * scale, 0.0), 0), (jnp.where(tall >= DH, raw, 0.0), 1)):
+            for lo, hi in tiles:
+                first, n = 2 * lo + side * (hi - lo), min(hi, unit) - lo
+                qdz[i, first:first + n] = value[lo:lo + n].astype(BF)
 
     def forth(j, i):
         for lo, hi in tiles:
@@ -640,28 +644,33 @@
         dsum_ref[i] = jnp.broadcast_to((mine[2] * a + yours[2] * b) * inv, whole)
 
     def back(j, i):
-        probs, dscores = [], []
-        for s in range(n_subs):
-            at = slice(s * sub, (s + 1) * sub)
-            factor = jnp.exp(tops[j, i, s] - top_ref[i]) * total_ref[i]
-            prob = sbuf[j, i, at].reshape(sub // 8, 8, QP) * factor[None]
-            dscore = prob * (dpbuf[j, i, at].reshape(sub // 8, 8, QP) - dsum_ref[i][None])
-            probs.append(prob.reshape(sub, QP).astype(BF))
-            dscores.append(dscore.reshape(sub, QP).astype(BF))
-        dscore = jnp.concatenate(dscores, axis=0)
-        added = dot(jnp.concatenate([dscore, jnp.concatenate(probs, axis=0)], axis=1), qdz[i])
-        acc[j] += added.reshape(group, rows, PAIR)
-        more = dot(kt[j], dscore)
-        if j < U - 1:
-            more = dqacc[...] + more
-        dqacc[...] = more
+        for lo, hi in tiles:
+            probs, dscores = [], []
+            for s in range(n_subs):
+                at = slice(s * sub, (s + 1) * sub)
+                factor = jnp.exp(tops[j, i, s, :, lo:hi] - top_ref[i, :, lo:hi]) * total_ref[i, :, lo:hi]
+                prob = sbuf[j, i, at, lo:hi].reshape(sub // 8, 8, hi - lo) * factor[None]
+                dprod = dpbuf[j, i, at, lo:hi].reshape(sub // 8, 8, hi - lo)
+                dscore = prob * (dprod - dsum_ref[i, :, lo:hi][None])
+                probs.append(prob.reshape(sub, hi - lo).astype(BF))
+                dscores.append(dscore.reshape(sub, hi - lo).astype(BF))
+            for first in range(0, n_subs, n_subs // cuts):
+                some = slice(first, first + n_subs // cuts)
+                both = [jnp.concatenate(x[some], axis=0) for x in (dscores, probs)]
+                added = dot(jnp.concatenate(both, axis=1), qdz[i, 2 * lo:2 * hi])
+                at = slice(first * group // n_subs, (first + n_subs // cuts) * group // n_subs)
+                acc[j, at] += added.reshape(group // cuts, rows, PAIR)
+            more = dot(kt[j], jnp.concatenate(dscores, axis=0))
+            if j < U - 1:
+                more = dqacc[i, :, lo:hi] + more
+            dqacc[i, :, lo:hi] = more
 
     def dq_copy(i, t):
         d, ff = around(t)
         return remote(dq_send.at[i * group + d * F + ff], dq_in.at[part, head], dq_ss.at[0], dq_rs.at[part], (ff, i * per + d))
 
     def ship_queries(i):
-        dqs[...] = jnp.concatenate([dqacc[...], jnp.zeros((DH, QP), F32)], axis=0).T
+        dqs[...] = jnp.concatenate([dqacc[i], jnp.zeros((DH, QP), F32)], axis=0).T
         for d in range(per):
             for g in range(F):
                 base = (d * F + g) * rows
@@ -711,15 +720,21 @@
                     take_queries(i)
             forth(j, i)
         give(i)
-    last = [remote_block(n) for n in range(U)] + [local(n) for n in reversed(range(U))]
-    for n, i in enumerate(last):
+    last = [jnp.where(edge, remote_block(U - 1 - n), remote_block(n)) for n in range(U)]
+    for i in last:
         meet(i)
         for j in reversed(range(U)):
             back(j, i)
-            if n == B - 1 and j:
-                ship_keys(j)
         ship_queries(i)
-    ship_keys(0)
+    mine = [local(n) for n in reversed(range(U))]
+    for i in mine:
+        meet(i)
+    for j in reversed(range(U)):
+        for i in mine:
+            back(j, i)
+            if j == 0:
+                ship_queries(i)
+        ship_keys(j)
 
     def sent(ref, sem):
         remote(ref, ref, sem.at[0], sem.at[0], (f, w)).wait_send()
@@ -778,7 +793,7 @@
             vm(U, unit, PAIR), vm(U, unit, PAIR), vm(U, DH, unit),
             vm(C, QP, PAIR), vm(C, QP, PAIR), vm(C, 2 * QP, PAIR),
             vf(U, C, unit, QP), vf(U, C, unit, QP), vf(U, per * F, rows, PAIR),
-            vf(DH, QP), vf(QP, PAIR),
+            vf(C, DH, QP), vf(QP, PAIR),
             vf(U, C, subs, 8, QP), vf(C, 8, QP), vf(C, 8, QP), vf(C, 8, QP),
             vf(C, stats, PAIR), vf(C, stats, PAIR),
             vm(heads, rows, PAIR), vm(C * per * F, half, PAIR),

time: 41 us -> 40.1 us (0.978)
  Pallas kernels: 40.2 us -> 39.3 us
    pallas_call x1, Pallas kernels: 38 us -> 37.2 us  [local_halves(): pl.pallas_call(functools.partial(halves, F, W), out_shape=(jax.ShapeDtype...]
where the time goes in v4:
time: 40.1 us; the launch traced here: 39.9 us
  Pallas kernels  39.3 us (98%)
  between operations  0.64 us (2%)
    pallas_call x1, Pallas kernels, local_halves(): pl.pallas_call(functools.partial(halves, F, W), out_shape=(jax.ShapeDtype...  37.2 us
    pallas_call x1, Pallas kernels, local_halves(): pl.pallas_call(both_halves, out_shape=(out, out, out), in_specs=[pl.Block...  2.14 us

profile of v4, /device:TPU:0, one launch (start us, length us, event | category | flops | bytes accessed | tf_op | source)
XLA Modules:
  0.0 39.9 jit_solution(9388198585367928920)
XLA Ops:
  0.6 37.2 %shard_map.85 = (bf16[2,16,40,128]{3,2,1,0:T(8,128)(2,1)}, bf16[16,72,128]{2,1,0:T(8,128)(2,1)}) custom-call(s32[2,4]{1,0:T(2,128)} %bitcast.1, s32[4]{0:T(128)} %reg_hbm.1, bf16[1,72,1024]{2,1,0:T(8,128)(2,1)} %q_hbm.1, bf16[1,72,1024]{2,1,0:T(8,128)(2,1)} %k_hbm.1, bf16[1,72,1024]{2,1,0:T(8,128)(2,1)} %v_hbm.1, bf16[1,72,1024]{2,1,0:T(8,128)(2,1)} %d_hbm.1), custom_call_target="tpu_custom_call" | custom-call | tf_op jit(solution)/shard_map/pallas_call | solution.py:784
  37.8 2.1 %shard_map.86 = (bf16[1,72,1024]{2,1,0:T(8,128)(2,1)}, bf16[1,72,1024]{2,1,0:T(8,128)(2,1)}, bf16[1,72,1024]{2,1,0:T(8,128)(2,1)}) custom-call(bf16[2,16,40,128]{3,2,1,0:T(8,128)(2,1)} %get-tuple-element.5.dq_in, bf16[16,72,128]{2,1,0:T(8,128)(2,1)} %get-tuple-element.6.fin_in), custom_call_target="tpu_custom_call" | custom-call | tf_op jit(solution)/shard_map/pallas_call | solution.py:806

commit v5 on v4

--- a/solution.py
+++ b/solution.py
@@ -502,7 +502,9 @@
     def _():
         knock(below, block0 + 1, d0, f)
 
-    send_block(block0, 1)
+    for copy in (kv_copy, qd_copy):
+        for t in range(1, group):
+            copy(block0, t).start()
     for n in range(1, B):
         @pl.when(block0 >= n)
         def _():
@@ -669,7 +671,7 @@
         d, ff = around(t)
         return remote(dq_send.at[i * group + d * F + ff], dq_in.at[part, head], dq_ss.at[0], dq_rs.at[part], (ff, i * per + d))
 
-    def ship_queries(i):
+    def ship_queries(i, own):
         dqs[...] = jnp.concatenate([dqacc[i], jnp.zeros((DH, QP), F32)], axis=0).T
         for d in range(per):
             for g in range(F):
@@ -677,14 +679,10 @@
                 dq_send[i * group + d * F + g] = jnp.concatenate(
                     [dqs[base:base + half, :DH], dqs[base + rows - half:base + rows, :DH]], axis=1).astype(BF)
 
-        @pl.when(i == block0)
-        def _():
+        if own:
             pltpu.make_async_copy(dq_send.at[i * group + d0 * F + f], dq_in.at[part, head], dq_rs.at[part]).start()
-
-        @pl.when(i != block0)
-        def _():
-            dq_copy(i, 0).start()
-        each(1, group, lambda t: dq_copy(i, t).start())
+        for t in range(1 if own else 0, group):
+            dq_copy(i, t).start()
 
     def fin_copy(j, t):
         d, ff = around(t)
@@ -695,7 +693,8 @@
         fin_send[j * group:(j + 1) * group] = acc[j].astype(BF)
         if j == 0:
             pltpu.make_async_copy(fin_send.at[d0 * F + f], fin_in.at[head], fin_rs.at[0]).start()
-        each(0 if j else 1, group, lambda t: fin_copy(j, t).start())
+        for t in range(0 if j else 1, group):
+            fin_copy(j, t).start()
 
     def local(n):
         return part * U + lax.rem(u0 + n, U)
@@ -720,20 +719,20 @@
                     take_queries(i)
             forth(j, i)
         give(i)
-    last = [jnp.where(edge, remote_block(U - 1 - n), remote_block(n)) for n in range(U)]
+    last = [remote_block(U - 1 - n) for n in range(U)]
     for i in last:
         meet(i)
         for j in reversed(range(U)):
             back(j, i)
-        ship_queries(i)
+        ship_queries(i, False)
     mine = [local(n) for n in reversed(range(U))]
     for i in mine:
         meet(i)
     for j in reversed(range(U)):
-        for i in mine:
+        for n, i in enumerate(mine):
             back(j, i)
             if j == 0:
-                ship_queries(i)
+                ship_queries(i, n == U - 1)
         ship_keys(j)
 
     def sent(ref, sem):
@@ -801,13 +800,15 @@
             pltpu.SemaphoreType.REGULAR, pltpu.SemaphoreType.REGULAR,
         ],
         compiler_params=pltpu.CompilerParams(
-            collective_id=0, has_side_effects=True, vmem_limit_bytes=60 * 2 ** 20),
-    )(partners.T, registers, queries, keys_in, values_in, grad_out)
+            collective_id=0, has_side_effects=True, vmem_limit_bytes=40 * 2 ** 20),
+    )(*[pltpu.with_memory_space_constraint(x, pltpu.HBM) for x in (
+        partners.T, registers, queries, keys_in, values_in, grad_out)])
     return pl.pallas_call(
         both_halves,
         out_shape=(out, out, out),
         in_specs=[pl.BlockSpec(memory_space=pltpu.VMEM)] * 2,
         out_specs=(pl.BlockSpec(memory_space=pltpu.VMEM),) * 3,
+        compiler_params=pltpu.CompilerParams(vmem_limit_bytes=8 * 2 ** 20),
     )(dq_heads, kv_heads)
 
 

time: 40.1 us -> 38.1 us (0.950)
  Pallas kernels: 39.3 us -> 37.3 us
    pallas_call x1, Pallas kernels: 2.14 us -> 1.14 us  [local_halves(): pl.pallas_call(both_halves, out_shape=(out, out, out), in_specs=[pl.Block...]
    pallas_call x1, Pallas kernels: 37.2 us -> 36.2 us  [local_halves(): pl.pallas_call(functools.partial(halves, F, W), out_shape=(jax.ShapeDtype...]
where the time goes in v5:
time: 38.1 us; the launch traced here: 37.9 us
  Pallas kernels  37.3 us (98%)
  between operations  0.64 us (2%)
    pallas_call x1, Pallas kernels, local_halves(): pl.pallas_call(functools.partial(halves, F, W), out_shape=(jax.ShapeDtype...  36.2 us
    pallas_call x1, Pallas kernels, local_halves(): pl.pallas_call(both_halves, out_shape=(out, out, out), in_specs=[pl.Block...  1.14 us

profile of v5, /device:TPU:0, one launch (start us, length us, event | category | flops | bytes accessed | tf_op | source)
XLA Modules:
  0.0 37.9 jit_solution(10254542502940694525)
XLA Ops:
  0.6 36.2 %shard_map.85 = (bf16[2,16,40,128]{3,2,1,0:T(8,128)(2,1)S(1)}, bf16[16,72,128]{2,1,0:T(8,128)(2,1)S(1)}) custom-call(s32[2,4]{1,0:T(2,128)} %bitcast.1, s32[4]{0:T(128)} %reg_hbm.1, bf16[1,72,1024]{2,1,0:T(8,128)(2,1)} %q_hbm.1, bf16[1,72,1024]{2,1,0:T(8,128)(2,1)} %k_hbm.1, bf16[1,72,1024]{2,1,0:T(8,128)(2,1)} %v_hbm.1, bf16[1,72,1024]{2,1,0:T(8,128)(2,1)} %d_hbm.1), custom_call_target="tpu_custom_call" | custom-call | tf_op jit(solution)/shard_map/pallas_call | solution.py:783
  36.8 1.1 %shard_map.86 = (bf16[1,72,1024]{2,1,0:T(8,128)(2,1)}, bf16[1,72,1024]{2,1,0:T(8,128)(2,1)}, bf16[1,72,1024]{2,1,0:T(8,128)(2,1)}) custom-call(bf16[2,16,40,128]{3,2,1,0:T(8,128)(2,1)S(1)} %get-tuple-element.5.dq_in, bf16[16,72,128]{2,1,0:T(8,128)(2,1)S(1)} %get-tuple-element.6.fin_in), custom_call_target="tpu_custom_call" | custom-call | tf_op jit(solution)/shard_map/pallas_call | solution.py:806

commit v6 on v5

--- a/solution.py
+++ b/solution.py
@@ -14,7 +14,7 @@
 SPLITS = 3
 UNIT = 640
 TILE = 256
-SUB = 96
+SUB = 144
 HIDDEN = -1e30
 BF = jnp.bfloat16
 F32 = jnp.float32
@@ -443,21 +443,21 @@
         d, ff = around(group - t)
         knock(barrier, block0, d, ff)
 
-    @pl.when(block0 > 0)
-    def _():
-        knock(barrier, block0 - 1, d0, f)
-
-    @pl.when(block0 < B - 1)
-    def _():
-        knock(barrier, block0 + 1, d0, f)
-
-    each(1, group, greet)
     loads = [pltpu.make_async_copy(src, dst, in_sem.at[n]) for n, (src, dst) in enumerate(
         ((k_hbm, k_ref), (v_hbm, v_ref), (q_hbm, q_ref), (d_hbm, d_ref), (part_hbm, part_ref), (reg_hbm, reg_ref)))]
     for load in loads:
         load.start()
 
-    for first, second, out in ((k_ref, v_ref, kv_send), (q_ref, d_ref, qd_send)):
+    @pl.when(block0 > 0)
+    def _():
+        knock(barrier, block0 - 1, d0, f)
+
+    @pl.when(block0 < B - 1)
+    def _():
+        knock(barrier, block0 + 1, d0, f)
+
+    each(1, group, greet)
+    def pack(first, second, out):
         for load in (loads.pop(0), loads.pop(0)):
             load.wait()
         for j in range(width // PAIR):
@@ -467,6 +467,19 @@
             out[2 * j] = jnp.concatenate([one[:, :DH], two[:, :DH]], axis=1)
             out[2 * j + 1] = jnp.concatenate([one[:, DH:], two[:, DH:]], axis=1)
 
+    pack(k_ref, v_ref, kv_send)
+    pl.semaphore_wait(barrier, group - 1 + jnp.where(block0 > 0, 1, 0) + jnp.where(block0 < B - 1, 1, 0))
+
+    @pl.when(block0 > 0)
+    def _():
+        knock(above, block0 - 1, d0, f)
+
+    @pl.when(block0 < B - 1)
+    def _():
+        knock(below, block0 + 1, d0, f)
+
+    pack(q_ref, d_ref, qd_send)
+
     def remote(src, dst, ss, rs, device):
         return pltpu.make_async_remote_copy(src_ref=src, dst_ref=dst, send_sem=ss, recv_sem=rs,
                                             device_id=device, device_id_type=MESH)
@@ -492,16 +505,6 @@
 
     pltpu.make_async_copy(kv_send.at[head], kv_in.at[u0, d0, f], kv_rs.at[u0]).start()
     pltpu.make_async_copy(qd_send.at[head], qd_in.at[block0, d0, f], qd_rs.at[block0]).start()
-    pl.semaphore_wait(barrier, group - 1 + jnp.where(block0 > 0, 1, 0) + jnp.where(block0 < B - 1, 1, 0))
-
-    @pl.when(block0 > 0)
-    def _():
-        knock(above, block0 - 1, d0, f)
-
-    @pl.when(block0 < B - 1)
-    def _():
-        knock(below, block0 + 1, d0, f)
-
     for copy in (kv_copy, qd_copy):
         for t in range(1, group):
             copy(block0, t).start()

time: 38.1 us -> 38.2 us (level)
  no operation moved by 1% of the time
where the time goes in v6:
time: 38.2 us; the launch traced here: 38 us
  Pallas kernels  37.4 us (98%)
  between operations  0.64 us (2%)
    pallas_call x1, Pallas kernels, local_halves(): pl.pallas_call(functools.partial(halves, F, W), out_shape=(jax.ShapeDtype...  36.2 us
    pallas_call x1, Pallas kernels, local_halves(): pl.pallas_call(both_halves, out_shape=(out, out, out), in_specs=[pl.Block...  1.14 us

profile of v6, /device:TPU:0, one launch (start us, length us, event | category | flops | bytes accessed | tf_op | source)
XLA Modules:
  0.0 38.0 jit_solution(17801726464430320337)
XLA Ops:
  0.6 36.2 %shard_map.85 = (bf16[2,16,40,128]{3,2,1,0:T(8,128)(2,1)S(1)}, bf16[16,72,128]{2,1,0:T(8,128)(2,1)S(1)}) custom-call(s32[2,4]{1,0:T(2,128)} %bitcast.1, s32[4]{0:T(128)} %reg_hbm.1, bf16[1,72,1024]{2,1,0:T(8,128)(2,1)} %q_hbm.1, bf16[1,72,1024]{2,1,0:T(8,128)(2,1)} %k_hbm.1, bf16[1,72,1024]{2,1,0:T(8,128)(2,1)} %v_hbm.1, bf16[1,72,1024]{2,1,0:T(8,128)(2,1)} %d_hbm.1), custom_call_target="tpu_custom_call" | custom-call | tf_op jit(solution)/shard_map/pallas_call | solution.py:786
  36.9 1.1 %shard_map.86 = (bf16[1,72,1024]{2,1,0:T(8,128)(2,1)}, bf16[1,72,1024]{2,1,0:T(8,128)(2,1)}, bf16[1,72,1024]{2,1,0:T(8,128)(2,1)}) custom-call(bf16[2,16,40,128]{3,2,1,0:T(8,128)(2,1)S(1)} %get-tuple-element.5.dq_in, bf16[16,72,128]{2,1,0:T(8,128)(2,1)S(1)} %get-tuple-element.6.fin_in), custom_call_target="tpu_custom_call" | custom-call | tf_op jit(solution)/shard_map/pallas_call | solution.py:809

commit v7 on v6

--- a/solution.py
+++ b/solution.py
@@ -723,19 +723,19 @@
             forth(j, i)
         give(i)
     last = [remote_block(U - 1 - n) for n in range(U)]
-    for i in last:
-        meet(i)
-        for j in reversed(range(U)):
-            back(j, i)
-        ship_queries(i, False)
-    mine = [local(n) for n in reversed(range(U))]
-    for i in mine:
-        meet(i)
+    i = last[0]
+    meet(i)
     for j in reversed(range(U)):
-        for n, i in enumerate(mine):
+        back(j, i)
+    ship_queries(i, False)
+    rest = last[1:] + [local(n) for n in reversed(range(U))]
+    for j in reversed(range(U)):
+        for n, i in enumerate(rest):
+            if j == U - 1:
+                meet(i)
             back(j, i)
             if j == 0:
-                ship_queries(i, n == U - 1)
+                ship_queries(i, n == len(rest) - 1)
         ship_keys(j)
 
     def sent(ref, sem):

time: 38.2 us -> 38.2 us (level)
  no operation moved by 1% of the time
where the time goes in v7:
time: 38.2 us; the launch traced here: 38.1 us
  Pallas kernels  37.5 us (98%)
  between operations  0.64 us (2%)
    pallas_call x1, Pallas kernels, local_halves(): pl.pallas_call(functools.partial(halves, F, W), out_shape=(jax.ShapeDtype...  36.3 us
    pallas_call x1, Pallas kernels, local_halves(): pl.pallas_call(both_halves, out_shape=(out, out, out), in_specs=[pl.Block...  1.14 us

profile of v7, /device:TPU:0, one launch (start us, length us, event | category | flops | bytes accessed | tf_op | source)
XLA Modules:
  0.0 38.1 jit_solution(3935503833120586473)
XLA Ops:
  0.6 36.3 %shard_map.85 = (bf16[2,16,40,128]{3,2,1,0:T(8,128)(2,1)S(1)}, bf16[16,72,128]{2,1,0:T(8,128)(2,1)S(1)}) custom-call(s32[2,4]{1,0:T(2,128)} %bitcast.1, s32[4]{0:T(128)} %reg_hbm.1, bf16[1,72,1024]{2,1,0:T(8,128)(2,1)} %q_hbm.1, bf16[1,72,1024]{2,1,0:T(8,128)(2,1)} %k_hbm.1, bf16[1,72,1024]{2,1,0:T(8,128)(2,1)} %v_hbm.1, bf16[1,72,1024]{2,1,0:T(8,128)(2,1)} %d_hbm.1), custom_call_target="tpu_custom_call" | custom-call | tf_op jit(solution)/shard_map/pallas_call | solution.py:786
  37.0 1.1 %shard_map.86 = (bf16[1,72,1024]{2,1,0:T(8,128)(2,1)}, bf16[1,72,1024]{2,1,0:T(8,128)(2,1)}, bf16[1,72,1024]{2,1,0:T(8,128)(2,1)}) custom-call(bf16[2,16,40,128]{3,2,1,0:T(8,128)(2,1)S(1)} %get-tuple-element.5.dq_in, bf16[16,72,128]{2,1,0:T(8,128)(2,1)S(1)} %get-tuple-element.6.fin_in), custom_call_target="tpu_custom_call" | custom-call | tf_op jit(solution)/shard_map/pallas_call | solution.py:809
